TPU v7x, 32 devices: a whole 2x2x4 slice. The times are simulated.
32 devices in a mesh: dp: 4 (over x, core), expert: 8 (over z, y).
Axes of the slice: x: 2, y: 2, z: 4, core: 2. Of those that a mesh axis runs over, the one named last changes fastest.
Arguments:
- patches: bfloat16 [3, 16384, 384], P(None, ('dp', 'expert')), may hold values from -6 to 6
- out_grad: bfloat16 [3, 16384, 384], P(None, ('dp', 'expert')), may hold values from -6 to 6
- item_ids: int32 [3, 32, 512], P(None, ('dp', 'expert')), may hold values from 0 to 7, never falling along the last dimension, each value on 1 to 128 neighbouring positions
- expert_ids: int32 [3, 16384, 2], P(None, ('dp', 'expert')), may hold values from 0 to 7, all different within a row; in each aligned block of 512 rows (0 to 511, 512 to 1023, ..., all dimensions but the last counted through in order) at most 256 rows name the same one
- qkv_master: float32 [384, 1152], replicated, may hold values from -0.3125 to 0.3125
- qkv_first: float32 [384, 1152], replicated
- qkv_second: float32 [384, 1152], replicated, as said below
- proj_master: float32 [384, 384], replicated, may hold values from -1.25 to 1.25
- proj_first: float32 [384, 384], replicated
- proj_second: float32 [384, 384], replicated, as said below
- router_master: float32 [384, 8], replicated, may hold values from -0.21875 to 0.21875
- router_first: float32 [384, 8], replicated
- router_second: float32 [384, 8], replicated, as said below
- gains_master: float32 [2, 384], replicated, may hold values from 0.5 to 1.5
- gains_first: float32 [2, 384], replicated
- gains_second: float32 [2, 384], replicated, as said below
- inner_master: float32 [8, 384, 1536], P('expert', 'dp'), may hold values from -0.3125 to 0.3125
- inner_first: float32 [8, 384, 1536], P('expert', 'dp')
- inner_second: float32 [8, 384, 1536], P('expert', 'dp'), as said below
- down_master: float32 [8, 768, 384], P('expert', 'dp'), may hold values from -0.4375 to 0.4375
- down_first: float32 [8, 768, 384], P('expert', 'dp')
- down_second: float32 [8, 768, 384], P('expert', 'dp'), as said below
Outputs:
- block_out: bfloat16 [3, 16384, 384], P(None, ('dp', 'expert'))
- patch_grad: float32 [3, 16384, 384], P(None, ('dp', 'expert'))
- qkv_updated: float32 [384, 1152], replicated
- qkv_first_new: float32 [384, 1152], replicated
- qkv_second_new: float32 [384, 1152], replicated
- proj_updated: float32 [384, 384], replicated
- proj_first_new: float32 [384, 384], replicated
- proj_second_new: float32 [384, 384], replicated
- router_updated: float32 [384, 8], replicated
- router_first_new: float32 [384, 8], replicated
- router_second_new: float32 [384, 8], replicated
- gains_updated: float32 [2, 384], replicated
- gains_first_new: float32 [2, 384], replicated
- gains_second_new: float32 [2, 384], replicated
- inner_updated: float32 [8, 384, 1536], P('expert', 'dp')
- inner_first_new: float32 [8, 384, 1536], P('expert', 'dp')
- inner_second_new: float32 [8, 384, 1536], P('expert', 'dp')
- down_updated: float32 [8, 768, 384], P('expert', 'dp')
- down_first_new: float32 [8, 768, 384], P('expert', 'dp')
- down_second_new: float32 [8, 768, 384], P('expert', 'dp')
Inputs may be any that keep to these rules, and one draw needn't show every extreme that they name: `expert_ids`: each row names 2 different experts. In each aligned block of 512 rows of a micro-batch (the rows of one device) no expert is named by more than 256 rows, and some expert reaches 256. `item_ids`: within each pack of 512 tokens the item numbers never fall; an item holds 1 to 128 tokens, and some item holds exactly 128. `qkv_second`: all entries positive. `proj_second`: all entries positive. `router_second`: all entries positive. `gains_second`: all entries positive. `inner_second`: all entries positive. `down_second`: all entries positive.
All inputs are finite; a program needn't handle non-finite values.
Results may differ from a plain program's by a relative error of at most 0.013.
The roundings to bfloat16 on the way count: a program that leaves them out, or rounds other values in their place, can miss the bound.
Values may be sent and summed in bfloat16 or wider, within the bound.
A program may use at most 128 MiB of HBM per device.

v0:
```python
import functools

import jax
import jax.numpy as jnp
import numpy as np
from jax import lax
from jax.experimental import pallas as pl
from jax.experimental.pallas import tpu as pltpu
from jax.sharding import PartitionSpec as P

HEADS = 6
HEAD = 64


norm_eps = 1e-06
adam_eps = 1e-08
correction = 0.875


def rotary_tables(item_row):
    length = item_row.shape[0]
    places = jnp.arange(length, dtype=jnp.int32)
    starts = jnp.concatenate([jnp.ones((1,), dtype=bool), item_row[1:] != item_row[:-1]])
    first = lax.cummax(jnp.where(starts, places, 0), axis=0)
    offset = (places - first).astype(jnp.float32)
    half = HEAD // 2
    freqs = 10000.0 ** (-jnp.arange(half, dtype=jnp.float32) / half)
    angles = offset[:, None] * freqs[None, :]
    return (jnp.cos(angles), jnp.sin(angles))


def rotate(vectors, cosine, sine):
    half = vectors.shape[-1] // 2
    first_half = vectors[..., :half]
    second_half = vectors[..., half:]
    cos_part = cosine[:, None, :]
    sin_part = sine[:, None, :]
    return jnp.concatenate(
        [
            first_half * cos_part - second_half * sin_part,
            second_half * cos_part + first_half * sin_part,
        ],
        axis=-1,
    )


def masked_scores(query, keys, same_item):
    scores = jnp.einsum("qhe,khe->hqk", query, keys, preferred_element_type=jnp.float32) * 0.125
    return jnp.where(same_item[None], scores, -1e30)


def adamw(weight, first, second, grad, rate, decay):
    first_new = 0.5 * first + 0.5 * grad
    second_new = 0.5 * second + 0.5 * grad * grad
    update = first_new / correction / (jnp.sqrt(second_new / correction) + adam_eps)
    return (weight - rate * (update + decay * weight), first_new, second_new)


def local(
    patches,
    out_grad,
    item_ids,
    expert_ids,
    qkv_master,
    qkv_first,
    qkv_second,
    proj_master,
    proj_first,
    proj_second,
    router_master,
    router_first,
    router_second,
    gains_master,
    gains_first,
    gains_second,
    inner_master,
    inner_first,
    inner_second,
    down_master,
    down_first,
    down_second,
):
    expert_count = lax.axis_size("expert")
    local_experts = inner_master.shape[0]
    experts = expert_count * local_experts
    length = patches.shape[1]
    width = patches.shape[2]
    top = expert_ids.shape[2]
    capacity = 2 * length * top // experts
    hidden_width = down_master.shape[1] * lax.axis_size("dp")
    inner_low, down_low = (
        lax.all_gather(inner_master.astype(jnp.bfloat16), "dp", axis=1, tiled=True),
        lax.all_gather(down_master.astype(jnp.bfloat16), "dp", axis=1, tiled=True),
    )
    qkv_low = qkv_master.astype(jnp.bfloat16)
    proj_low = proj_master.astype(jnp.bfloat16)
    router_low = router_master.astype(jnp.bfloat16)
    gain_attn = gains_master[0]
    gain_ffn = gains_master[1]
    expert_numbers = jnp.arange(experts, dtype=jnp.int32)

    def expert_forward(received):
        count = received.shape[1]
        grid = received.reshape(expert_count, local_experts, count, width)
        both = jnp.einsum("sjcd,jdf->sjcf", grid, inner_low, preferred_element_type=jnp.float32)
        hidden = (jax.nn.silu(both[..., :hidden_width]) * both[..., hidden_width:]).astype(
            jnp.bfloat16
        )
        result = jnp.einsum("sjcf,jfd->sjcd", hidden, down_low, preferred_element_type=jnp.float32)
        result = result.astype(jnp.bfloat16).reshape(experts, count, width)
        returned = lax.all_to_all(result, "expert", split_axis=0, concat_axis=0, tiled=True)
        return (returned, received)

    def micro_step(carry, inputs):
        grad_qkv, grad_proj, grad_router, grad_gains, grad_inner, grad_down = carry
        patch, upstream, item_block, routes = inputs
        items = item_block[0]
        source = patch.astype(jnp.float32)
        inv_first = lax.rsqrt(jnp.mean(source * source, axis=1, keepdims=True) + norm_eps)
        unit_first = source * inv_first
        normed_in = (unit_first * gain_attn).astype(jnp.bfloat16)
        mixed = jnp.dot(normed_in, qkv_low, preferred_element_type=jnp.float32)
        cosine, sine = rotary_tables(items)
        query = rotate(mixed[:, :width].reshape(length, HEADS, HEAD), cosine, sine).astype(
            jnp.bfloat16
        )
        keys = rotate(
            mixed[:, width : 2 * width].reshape(length, HEADS, HEAD), cosine, sine
        ).astype(jnp.bfloat16)
        values = mixed[:, 2 * width :].reshape(length, HEADS, HEAD).astype(jnp.bfloat16)
        same_item = items[:, None] == items[None, :]
        scores = masked_scores(query, keys, same_item)
        peak = jnp.max(scores, axis=2, keepdims=True)
        weights = jnp.exp(scores - peak)
        totals = jnp.sum(weights, axis=2, keepdims=True)
        probs_low = (weights / totals).astype(jnp.bfloat16)
        log_total = peak + jnp.log(totals)
        attended = jnp.einsum("hqk,khe->qhe", probs_low, values, preferred_element_type=jnp.float32)
        attended = attended.reshape(length, width).astype(jnp.bfloat16)
        middle = source + jnp.dot(attended, proj_low, preferred_element_type=jnp.float32)
        inv_second = lax.rsqrt(jnp.mean(middle * middle, axis=1, keepdims=True) + norm_eps)
        unit_second = middle * inv_second
        normed_mid = (unit_second * gain_ffn).astype(jnp.bfloat16)
        logits = jnp.dot(normed_mid, router_low, preferred_element_type=jnp.float32)
        chosen = jnp.take_along_axis(logits, routes, axis=1)
        gates = jax.nn.softmax(chosen, axis=1)
        flat_ids = routes.reshape(length * top)
        hits = (flat_ids[:, None] == expert_numbers[None, :]).astype(jnp.int32)
        rank = jnp.sum(jnp.cumsum(hits, axis=0) * hits, axis=1) - 1
        slots = flat_ids * capacity + rank
        copies = jnp.repeat(normed_mid, top, axis=0)
        outgoing = jnp.zeros((experts * capacity, width), jnp.bfloat16).at[slots].set(copies)
        outgoing = outgoing.reshape(experts, capacity, width)
        returned, kept_inputs = expert_forward(
            lax.all_to_all(outgoing, "expert", split_axis=0, concat_axis=0, tiled=True)
        )
        picked = (
            returned.reshape(experts * capacity, width)[slots]
            .reshape(length, top, width)
            .astype(jnp.float32)
        )
        combined = jnp.sum(gates[:, :, None] * picked, axis=1)
        block_out = (middle + combined).astype(jnp.bfloat16)
        upstream_full = upstream.astype(jnp.float32)
        grad_gate = jnp.sum(upstream_full[:, None, :] * picked, axis=2)
        grad_chosen = gates * (grad_gate - jnp.sum(gates * grad_gate, axis=1, keepdims=True))
        route_hits = (routes[:, :, None] == expert_numbers[None, None, :]).astype(jnp.float32)
        grad_logits = jnp.sum(grad_chosen[:, :, None] * route_hits, axis=1).astype(jnp.bfloat16)
        grad_router_now = jnp.dot(normed_mid.T, grad_logits, preferred_element_type=jnp.float32)
        grad_mid = jnp.dot(grad_logits, router_low.T, preferred_element_type=jnp.float32)
        grad_slots = (
            (gates[:, :, None] * upstream_full[:, None, :])
            .astype(jnp.bfloat16)
            .reshape(length * top, width)
        )
        grad_outgoing = (
            jnp.zeros((experts * capacity, width), jnp.bfloat16).at[slots].set(grad_slots)
        )
        grad_outgoing = grad_outgoing.reshape(experts, capacity, width)
        incoming, inputs_back = (
            lax.all_to_all(grad_outgoing, "expert", split_axis=0, concat_axis=0, tiled=True),
            lax.all_to_all(outgoing, "expert", split_axis=0, concat_axis=0, tiled=True),
        )
        grid_in = inputs_back.reshape(expert_count, local_experts, capacity, width)
        grid_grad = incoming.reshape(expert_count, local_experts, capacity, width)
        both = jnp.einsum("sjcd,jdf->sjcf", grid_in, inner_low, preferred_element_type=jnp.float32)
        gate_part = both[..., :hidden_width]
        up_part = both[..., hidden_width:]
        sigma = jax.nn.sigmoid(gate_part)
        activated = jax.nn.silu(gate_part)
        hidden = (activated * up_part).astype(jnp.bfloat16)
        grad_hidden = jnp.einsum(
            "sjcd,jfd->sjcf", grid_grad, down_low, preferred_element_type=jnp.float32
        )
        grad_down_now = jnp.einsum(
            "sjcf,sjcd->jfd", hidden, grid_grad, preferred_element_type=jnp.float32
        )
        grad_both = jnp.concatenate(
            [
                grad_hidden * up_part * sigma * (1.0 + gate_part * (1.0 - sigma)),
                grad_hidden * activated,
            ],
            axis=3,
        ).astype(jnp.bfloat16)
        grad_inner_now = jnp.einsum(
            "sjcd,sjcf->jdf", grid_in, grad_both, preferred_element_type=jnp.float32
        )
        grad_copies = jnp.einsum(
            "sjcf,jdf->sjcd", grad_both, inner_low, preferred_element_type=jnp.float32
        )
        grad_copies = grad_copies.astype(jnp.bfloat16).reshape(experts, capacity, width)
        grad_back = lax.all_to_all(grad_copies, "expert", split_axis=0, concat_axis=0, tiled=True)
        grad_picked = grad_back.reshape(experts * capacity, width)[slots].reshape(
            length, top, width
        )
        grad_mid = grad_mid + jnp.sum(grad_picked.astype(jnp.float32), axis=1)
        grad_unit_second = grad_mid * gain_ffn
        grad_gain_ffn = jnp.sum(grad_mid * unit_second, axis=0)
        grad_middle = upstream_full + inv_second * (
            grad_unit_second
            - unit_second * jnp.mean(grad_unit_second * unit_second, axis=1, keepdims=True)
        )
        grad_branch = grad_middle.astype(jnp.bfloat16)
        grad_proj_now = jnp.dot(attended.T, grad_branch, preferred_element_type=jnp.float32)
        grad_attended = jnp.dot(grad_branch, proj_low.T, preferred_element_type=jnp.float32)
        grad_attended = grad_attended.astype(jnp.bfloat16).reshape(length, HEADS, HEAD)
        probs_again = jnp.exp(masked_scores(query, keys, same_item) - log_total)
        grad_probs = jnp.einsum(
            "qhe,khe->hqk", grad_attended, values, preferred_element_type=jnp.float32
        )
        grad_values = jnp.einsum(
            "hqk,qhe->khe", probs_low, grad_attended, preferred_element_type=jnp.float32
        )
        grad_scores = probs_again * (
            grad_probs - jnp.sum(probs_again * grad_probs, axis=2, keepdims=True)
        )
        grad_scores = grad_scores.astype(jnp.bfloat16)
        grad_query = (
            jnp.einsum("hqk,khe->qhe", grad_scores, keys, preferred_element_type=jnp.float32)
            * 0.125
        )
        grad_keys = (
            jnp.einsum("hqk,qhe->khe", grad_scores, query, preferred_element_type=jnp.float32)
            * 0.125
        )
        grad_mixed = jnp.concatenate(
            [
                rotate(grad_query, cosine, -sine).reshape(length, width),
                rotate(grad_keys, cosine, -sine).reshape(length, width),
                grad_values.reshape(length, width),
            ],
            axis=1,
        ).astype(jnp.bfloat16)
        grad_qkv_now = jnp.dot(normed_in.T, grad_mixed, preferred_element_type=jnp.float32)
        grad_normed = jnp.dot(grad_mixed, qkv_low.T, preferred_element_type=jnp.float32)
        grad_unit_first = grad_normed * gain_attn
        grad_gain_attn = jnp.sum(grad_normed * unit_first, axis=0)
        patch_grad = grad_middle + inv_first * (
            grad_unit_first
            - unit_first * jnp.mean(grad_unit_first * unit_first, axis=1, keepdims=True)
        )
        new_carry = (
            grad_qkv + grad_qkv_now,
            grad_proj + grad_proj_now,
            grad_router + grad_router_now,
            grad_gains + jnp.stack([grad_gain_attn, grad_gain_ffn]),
            grad_inner + grad_inner_now,
            grad_down + grad_down_now,
        )
        return (new_carry, (block_out, patch_grad))

    start = (
        jnp.zeros(qkv_master.shape, jnp.float32),
        jnp.zeros(proj_master.shape, jnp.float32),
        jnp.zeros(router_master.shape, jnp.float32),
        jnp.zeros(gains_master.shape, jnp.float32),
        jnp.zeros(inner_low.shape, jnp.float32),
        jnp.zeros(down_low.shape, jnp.float32),
    )
    totals, outputs = lax.scan(micro_step, start, (patches, out_grad, item_ids, expert_ids))
    grad_qkv, grad_proj, grad_router, grad_gains = lax.psum(
        (totals[0], totals[1], totals[2], totals[3]), ("dp", "expert")
    )
    grad_inner, grad_down = (
        lax.psum_scatter(totals[4], "dp", scatter_dimension=1, tiled=True),
        lax.psum_scatter(totals[5], "dp", scatter_dimension=1, tiled=True),
    )
    qkv_new = adamw(qkv_master, qkv_first, qkv_second, grad_qkv, 0.1, 0.1)
    proj_new = adamw(proj_master, proj_first, proj_second, grad_proj, 0.4, 0.1)
    router_new = adamw(router_master, router_first, router_second, grad_router, 0.07, 0.1)
    gains_new = adamw(gains_master, gains_first, gains_second, grad_gains, 0.4, 0.0)
    inner_new = adamw(inner_master, inner_first, inner_second, grad_inner, 0.1, 0.1)
    down_new = adamw(down_master, down_first, down_second, grad_down, 0.15, 0.1)
    return (
        outputs[0],
        outputs[1],
        qkv_new[0],
        qkv_new[1],
        qkv_new[2],
        proj_new[0],
        proj_new[1],
        proj_new[2],
        router_new[0],
        router_new[1],
        router_new[2],
        gains_new[0],
        gains_new[1],
        gains_new[2],
        inner_new[0],
        inner_new[1],
        inner_new[2],
        down_new[0],
        down_new[1],
        down_new[2],
    )


F32 = jnp.float32
BF16 = jnp.bfloat16
QB = 128


def iota(shape, axis):
    return lax.broadcasted_iota(jnp.int32, shape, axis)


def dot_nn(a, b):
    return jnp.dot(a, b, preferred_element_type=F32)


def dot_nt(a, b):
    return lax.dot_general(a, b, (((1,), (1,)), ((), ())), preferred_element_type=F32)


def dot_tn(a, b):
    return lax.dot_general(a, b, (((0,), (0,)), ((), ())), preferred_element_type=F32)


def swap_halves(v, low_lane):
    width = v.shape[1]
    half = HEAD // 2
    return jnp.where(low_lane, pltpu.roll(v, width - half, 1), pltpu.roll(v, half, 1))


def turn(v, cos_row, sin_row, low_lane):
    return v * cos_row + swap_halves(v, low_lane) * sin_row


def rope_table(item_max):
    half = HEAD // 2
    offset = np.arange(item_max, dtype=np.float32)
    freqs = np.float32(10000.0) ** (-np.arange(half, dtype=np.float32) / np.float32(half))
    angles = (offset[:, None] * freqs[None, :]).astype(np.float32)
    cosine, sine = np.cos(angles), np.sin(angles)
    return np.concatenate([cosine] * 4 + [-sine, sine] * 2, axis=1).astype(np.float32)


def windows(length):
    found = []
    for start in range(0, length, QB):
        low = max(0, start - QB)
        high = min(length, start + 2 * QB)
        found.append((start, low, high))
    return found


def row_norm(values):
    return lax.rsqrt(jnp.mean(values * values, axis=1, keepdims=True) + norm_eps)


def positions(item_row, length):
    eye = iota((length, length), 0) == iota((length, length), 1)
    col = jnp.sum(jnp.where(eye, item_row, 0.0), axis=1, keepdims=True)
    before = jnp.sum(jnp.where(item_row < col, 1.0, 0.0), axis=1, keepdims=True)
    offset = iota((length, 1), 0) - before.astype(jnp.int32)
    return col, offset


def rope_rows(offset, table, length, width):
    spots = table.shape[0]
    pick = jnp.where(iota((length, spots), 1) == offset, 1.0, 0.0)
    both = jnp.dot(pick, table, precision=lax.Precision.HIGHEST, preferred_element_type=F32)
    copies = width // 128
    return (
        jnp.concatenate([both[:, :128]] * copies, axis=1),
        jnp.concatenate([both[:, 128:]] * copies, axis=1),
    )


VMEM_BYTES = 64 * 1024 * 1024 - 512 * 1024


MESH_ID = pl.DeviceIdType.MESH


class Place:
    def __init__(self, line):
        self.line = line
        dp, ex = lax.axis_index("dp"), lax.axis_index("expert")
        self.x, self.core = lax.div(dp, 2), lax.rem(dp, 2)
        self.z, self.y = lax.div(ex, 2), lax.rem(ex, 2)

    def device(self, flip_x=0, flip_y=0, flip_core=0, z=None):
        x = 1 - self.x if flip_x else self.x
        y = 1 - self.y if flip_y else self.y
        core = 1 - self.core if flip_core else self.core
        return (2 * x + core, 2 * (self.z if z is None else z) + y)

    def levels(self):
        found = [(0, self.z, None, 0)]
        for away in range(1, self.line):
            found.append((away, self.z - away, lambda a=away: self.z >= a, -1))
            found.append((away, self.z + away, lambda a=away: self.z + a < self.line, 1))
        return found

    def up(self):
        return self.z + 1 < self.line

    def down(self):
        return self.z > 0

    def by_distance(self, i):
        found = 0
        for z in range(self.line):
            order = sorted(range(self.line), key=lambda level: (abs(level - z), level))
            for place, level in enumerate(order):
                hit = jnp.logical_and(self.z == z, i == place).astype(jnp.int32)
                found = found + hit * level
        return found

    def greet(self):
        barrier = pltpu.get_barrier_semaphore()

        def signal(device):
            pl.semaphore_signal(barrier, inc=1, device_id=device, device_id_type=MESH_ID)

        for device in (self.device(1), self.device(0, 1), self.device(0, 0, 1)):
            signal(device)
        for step in range(1, self.line):
            signal(self.device(z=lax.rem(self.z + step, self.line)))
        pl.semaphore_wait(barrier, self.line + 2)


def both(*tests):
    tests = [t for t in tests if t is not None]

    def all_of():
        found = tests[0]()
        for t in tests[1:]:
            found = jnp.logical_and(found, t())
        return found

    return all_of if tests else None


def only(test, body):
    if test is None:
        body()
    else:
        pl.when(test())(body)


def remote(source, target, departure, arrival, device):
    return pltpu.make_async_remote_copy(
        src_ref=source,
        dst_ref=target,
        send_sem=departure,
        recv_sem=arrival,
        device_id=device,
        device_id_type=MESH_ID,
    )


class Wires:
    def __init__(self, send_sem, like):
        self.send_sem, self.like = send_sem, like
        self.sent = []

    def send(self, source, target, arrival, device, test=None):
        copy = pltpu.make_async_remote_copy(
            src_ref=source,
            dst_ref=target,
            send_sem=self.send_sem.at[len(self.sent)],
            recv_sem=arrival,
            device_id=device,
            device_id_type=MESH_ID,
        )
        only(test, copy.start)
        self.sent.append(test)

    def arrived(self, target, arrival, device, test=None):
        copy = pltpu.make_async_remote_copy(
            src_ref=target,
            dst_ref=target,
            send_sem=self.send_sem.at[0],
            recv_sem=arrival,
            device_id=device,
            device_id_type=MESH_ID,
        )
        only(test, copy.wait_recv)

    def finish(self):
        for number, test in enumerate(self.sent):
            copy = pltpu.make_async_remote_copy(
                src_ref=self.like,
                dst_ref=self.like,
                send_sem=self.send_sem.at[number],
                recv_sem=self.send_sem.at[number],
                device_id=(0, 0),
                device_id_type=MESH_ID,
            )
            only(test, copy.wait_send)


class Gather:
    def __init__(self, place, shard, full, send_sem, recv_sem, copy_sem):
        self.place, self.shard, self.full = place, shard, full
        self.recv_sem, self.copy_sem = recv_sem, copy_sem
        self.wires = Wires(send_sem, shard)

    def at(self, device):
        return self.full.at[device[1], device[0]]

    def ready(self, device):
        return self.recv_sem.at[device[1], device[0]]

    def pass_on(self, origin, to, test=None, source=None):
        source = self.at(origin) if source is None else source
        self.wires.send(source, self.at(origin), self.ready(origin), to, test)

    def wait(self, origin, test=None):
        self.wires.arrived(self.at(origin), self.ready(origin), self.place.device(0, 0, 1), test)

    def start(self):
        place = self.place
        me = place.device()
        self.pass_on(me, place.device(z=place.z + 1), place.up, self.shard)
        self.pass_on(me, place.device(z=place.z - 1), place.down, self.shard)
        self.pass_on(me, place.device(1), None, self.shard)
        self.pass_on(me, place.device(0, 1), None, self.shard)
        self.pass_on(me, place.device(0, 0, 1), None, self.shard)
        self.own = pltpu.make_async_copy(self.shard, self.at(me), self.copy_sem)
        self.own.start()

    def column(self, away):
        place = self.place
        for dist, level, test, way in place.levels():
            if dist != away:
                continue
            origin = place.device(z=level)
            self.wait(origin, test)
            if way < 0:
                self.pass_on(origin, place.device(z=place.z + 1), both(test, place.up))
            if way > 0:
                self.pass_on(origin, place.device(z=place.z - 1), both(test, place.down))
            self.pass_on(origin, place.device(1), test)
            self.pass_on(origin, place.device(0, 1), test)
            self.pass_on(origin, place.device(0, 0, 1), test)

    def square(self, away):
        place = self.place
        for dist, level, test, way in place.levels():
            if dist != away:
                continue
            over_x, over_y = place.device(1, z=level), place.device(0, 1, z=level)
            self.wait(over_x, test)
            if dist % 2 == 0:
                self.pass_on(over_x, place.device(0, 1), test)
            self.pass_on(over_x, place.device(0, 0, 1), test)
            self.wait(over_y, test)
            if dist % 2 == 1:
                self.pass_on(over_y, place.device(1), test)
            self.pass_on(over_y, place.device(0, 0, 1), test)

    def corner(self, away):
        place = self.place
        for dist, level, test, way in place.levels():
            if dist != away:
                continue
            across = place.device(1, 1, z=level)
            self.wait(across, test)
            self.pass_on(across, place.device(0, 0, 1), test)

    def partner(self, flip_x, flip_y, level):
        self.wait(self.place.device(flip_x, flip_y, 1, z=level))


OWN, OVER_X, OVER_Y, ACROSS = 0, 1, 2, 3
FLIPS = ((0, 0), (1, 0), (0, 1), (1, 1))


class Reduce:
    def __init__(self, place, part, sums, core_in, diag_in, side_in, line_in, send_sem, recv, copy_sem):
        self.place, self.part, self.sums = place, part, sums
        self.core_in, self.diag_in, self.side_in, self.line_in = core_in, diag_in, side_in, line_in
        self.core_sem, self.diag_sem, self.side_sem, self.line_sem = recv
        self.copy_sem = copy_sem
        self.wires = Wires(send_sem, core_in.at[0, 0])

    def shard(self, group, level, flip_core=0):
        device = self.place.device(*FLIPS[group], flip_core, z=level)
        return self.part.at[device[1], device[0]]

    def pick(self, away):
        return [(level, test, way) for dist, level, test, way in self.place.levels() if dist == away]

    def share(self, group, away):
        for level, test, way in self.pick(away):
            load = pltpu.make_async_copy(
                self.shard(group, level), self.sums.at[group, level], self.copy_sem.at[group, level]
            )
            only(test, load.start)
            self.wires.send(
                self.shard(group, level, 1),
                self.core_in.at[group, level],
                self.core_sem.at[group, level],
                self.place.device(0, 0, 1),
                test,
            )

    def add(self, group, level, value):
        self.sums[group, level] = (self.sums[group, level].astype(F32) + value.astype(F32)).astype(BF16)

    def merge(self, group, away):
        place = self.place
        for level, test, way in self.pick(away):

            def body(level=level):
                pltpu.make_async_copy(
                    self.shard(group, level), self.sums.at[group, level], self.copy_sem.at[group, level]
                ).wait()
                self.wires.arrived(
                    self.core_in.at[group, level],
                    self.core_sem.at[group, level],
                    place.device(0, 0, 1),
                )
                self.add(group, level, self.core_in[group, level])

            only(test, body)

    def send_across(self, away):
        place = self.place
        side = OVER_Y if away % 2 == 0 else OVER_X
        for level, test, way in self.pick(away):
            self.wires.send(
                self.sums.at[ACROSS, level],
                self.diag_in.at[level],
                self.diag_sem.at[level],
                place.device(*FLIPS[side]),
                test,
            )

    def send_side(self, away):
        place = self.place
        group = OVER_X if away % 2 == 0 else OVER_Y
        for level, test, way in self.pick(away):

            def body(level=level):
                self.wires.arrived(self.diag_in.at[level], self.diag_sem.at[level], place.device(1))
                self.add(group, level, self.diag_in[level])

            only(test, body)
            for side in (OVER_X, OVER_Y):
                self.wires.send(
                    self.sums.at[side, level],
                    self.side_in.at[side - 1, level],
                    self.side_sem.at[side - 1, level],
                    place.device(*FLIPS[side]),
                    test,
                )

    def collect(self, level, test):
        place = self.place

        def body():
            total = self.sums[OWN, level].astype(F32)
            for side in range(2):
                self.wires.arrived(
                    self.side_in.at[side, level], self.side_sem.at[side, level], place.device(1)
                )
                total = total + self.side_in[side, level].astype(F32)
            self.sums[OWN, level] = total.astype(BF16)

        only(test, body)

    def send_line(self, away):
        place = self.place
        for level, test, way in self.pick(away):
            self.collect(level, test)
            lane = 0 if way < 0 else 1

            def body(level=level, lane=lane):
                self.wires.arrived(
                    self.line_in.at[lane, level], self.line_sem.at[lane, level], place.device(1)
                )
                self.add(OWN, level, self.line_in[lane, level])

            only(both(test, place.up if way < 0 else place.down), body)
            self.wires.send(
                self.sums.at[OWN, level],
                self.line_in.at[lane, level],
                self.line_sem.at[lane, level],
                place.device(z=place.z + way),
                test,
            )

    def finish(self, out):
        place = self.place
        level = place.z
        total = self.sums[OWN, level].astype(F32)
        for side in range(2):
            self.wires.arrived(
                self.side_in.at[side, level], self.side_sem.at[side, level], place.device(1)
            )
            total = total + self.side_in[side, level].astype(F32)
        out[...] = total
        for way, far in ((0, place.up), (1, place.down)):

            def body(way=way):
                self.wires.arrived(
                    self.line_in.at[way, level], self.line_sem.at[way, level], place.device(1)
                )
                out[...] += self.line_in[way, level].astype(F32)

            only(far, body)
        self.wires.finish()


EARLY = 1


class Close:
    def __init__(self, place, kept, owns, sides, diag_in, side_in, line_in, load_sem, sems):
        self.place, self.kept, self.owns, self.sides = place, kept, owns, sides
        self.diag_in, self.side_in, self.line_in, self.load_sem = diag_in, side_in, line_in, load_sem
        self.diag_send, self.diag_sem, self.side_send, self.side_sem, self.line_send, self.line_sem = sems

    def level(self, slot):
        return self.place.by_distance(self.place.line - 1 - slot)

    def load(self, which, slot):
        target = self.owns if which == 0 else self.sides
        return pltpu.make_async_copy(
            self.kept.at[which, self.level(slot)], target.at[slot], self.load_sem.at[which, slot]
        )

    def across(self, slot):
        level = self.level(slot)
        return remote(
            self.kept.at[2, level], self.diag_in.at[slot], self.diag_send.at[slot], self.diag_sem.at[slot],
            self.place.device(1),
        )

    def aside(self, slot):
        level = self.level(slot)
        source = self.kept.at[1, level] if slot < EARLY else self.sides.at[slot]
        return remote(
            source, self.side_in.at[slot], self.side_send.at[slot], self.side_sem.at[slot],
            self.place.device(0, 1),
        )

    def along(self, slot):
        return remote(
            self.owns.at[slot], self.line_in.at[self.place.z], self.line_send.at[slot],
            self.line_sem.at[self.place.z], self.place.device(z=self.level(slot)),
        )

    def start(self):
        for slot in range(self.place.line):
            (self.aside(slot) if slot < EARLY else self.across(slot)).start()
            self.load(0, slot).start()
            if slot >= EARLY:
                self.load(1, slot).start()

    def send_side(self, slot):
        self.load(1, slot).wait()
        self.across(slot).wait_recv()
        self.sides[slot] = (self.sides[slot].astype(F32) + self.diag_in[slot].astype(F32)).astype(BF16)
        self.aside(slot).start()

    def collect(self, slot):
        self.load(0, slot).wait()
        self.aside(slot).wait_recv()
        return self.owns[slot].astype(F32) + self.side_in[slot].astype(F32)

    def send_line(self, slot):
        self.owns[slot] = self.collect(slot).astype(BF16)
        self.along(slot).start()

    def finish(self, out):
        place = self.place
        last = place.line - 1
        out[...] = self.collect(last)
        for step in range(1, place.line):
            z = lax.rem(place.z + step, place.line)
            remote(
                self.owns.at[0], self.line_in.at[z], self.line_send.at[0], self.line_sem.at[z],
                place.device(z=z),
            ).wait_recv()
            out[...] += self.line_in[z].astype(F32)
        for slot in range(place.line):
            self.aside(slot).wait_send()
            if slot >= EARLY:
                self.across(slot).wait_send()
            if slot < last:
                self.along(slot).wait_send()


def copy_all(copies):
    for copy in copies:
        copy.start()


def attend_pack(p, patches, items, gains, table, qkv_s, proj_s, mixed_s, probs_s, att_s, mid_s, nm_s):
    _, length, width = patches.shape
    pairs = width // 128
    slot = lax.rem(p, mixed_s.shape[0])
    low_lane = iota((1, width), 1) % HEAD < HEAD // 2
    first_head = iota((1, 128), 1) < HEAD
    mask_a = jnp.where(first_head, 1.0, 0.0).astype(BF16)
    mask_b = jnp.where(first_head, 0.0, 1.0).astype(BF16)
    top_rows = iota((128, 1), 0) < HEAD
    source = patches[p].astype(F32)
    normed = (source * row_norm(source) * gains[0:1, :]).astype(BF16)
    mixed = dot_nn(normed, qkv_s[...])
    item_row = items[p].astype(F32)
    item_col, offset = positions(item_row, length)
    cos_row, sin_row = rope_rows(offset, table[...], length, width)
    mixed_s[slot, :, :width] = turn(mixed[:, :width], cos_row, sin_row, low_lane).astype(BF16)
    mixed_s[slot, :, width : 2 * width] = turn(
        mixed[:, width : 2 * width], cos_row, sin_row, low_lane
    ).astype(BF16)
    mixed_s[slot, :, 2 * width :] = mixed[:, 2 * width :].astype(BF16)
    for pair in range(pairs):
        lanes = slice(128 * pair, 128 * pair + 128)
        key_lanes = slice(width + 128 * pair, width + 128 * pair + 128)
        values_t = mixed[:, 2 * width + 128 * pair : 2 * width + 128 * pair + 128].T.astype(BF16)
        for block, (start, low, high) in enumerate(windows(length)):
            query = mixed_s[slot, start : start + QB, lanes] * 0.125
            query = jnp.concatenate([query * mask_a, query * mask_b], axis=0)
            scores = dot_nt(mixed_s[slot, low:high, key_lanes], query)
            here = item_row[:, start : start + QB]
            same = item_col[low:high] == jnp.concatenate([here, here], axis=1)
            scores = jnp.where(same, scores, -1e30)
            peak = jnp.max(scores, axis=0, keepdims=True)
            weights = jnp.exp(scores - peak)
            total = jnp.sum(weights, axis=0, keepdims=True)
            probs = (weights * (1.0 / total)).astype(BF16)
            probs_s[p, pair, block, : high - low] = probs
            out = dot_nn(values_t[:, low:high], probs)
            out = jnp.where(top_rows, out[:, :QB], out[:, QB:])
            att_s[p, start : start + QB, lanes] = out.T.astype(BF16)
    middle = source + dot_nn(att_s[p], proj_s[...])
    mid_s[p] = middle
    nm_s[p] = (middle * row_norm(middle) * gains[1:2, :]).astype(BF16)


class Experts:
    def __init__(self, refs, cap):
        (
            self.nm, self.upstream, self.rank_s, self.gate_s, self.gg_s, self.x_s, self.hid_s, self.go_s,
            self.gb_s, self.y_s, self.inner_w, self.down_w,
        ) = refs
        self.cap = cap

    def prepare(self, p, ids, router_w):
        nm = self.nm
        _, length, width = nm.shape
        experts = router_w.shape[0]
        earlier = jnp.where(iota((length, length), 0) < iota((length, length), 1), 1.0, 0.0).astype(BF16)
        logits = dot_nt(router_w[...], nm[p])
        number = iota((experts, length), 0)
        hit0 = number == ids[p, 0:1, :]
        hit1 = number == ids[p, 1:2, :]
        chosen0 = jnp.sum(jnp.where(hit0, logits, 0.0), axis=0, keepdims=True)
        chosen1 = jnp.sum(jnp.where(hit1, logits, 0.0), axis=0, keepdims=True)
        peak = jnp.maximum(chosen0, chosen1)
        e0 = jnp.exp(chosen0 - peak)
        e1 = jnp.exp(chosen1 - peak)
        total = e0 + e1
        self.gate_s[p] = jnp.where(hit0, e0 / total, 0.0) + jnp.where(hit1, e1 / total, 0.0)
        named = jnp.where(hit0, 1.0, jnp.where(hit1, 1.0, 0.0))
        rank = dot_nn(named.astype(BF16), earlier)
        self.rank_s[p] = jnp.where(named > 0.5, rank, -1.0)

    def rows(self, p, expert):
        cap = self.cap
        _, length, width = self.nm.shape
        hidden_width = self.hid_s.shape[1]
        here = pl.ds(pl.multiple_of(p * cap, cap), cap)
        rank = self.rank_s[p, pl.ds(expert, 1), :]
        gate_row = self.gate_s[p, pl.ds(expert, 1), :]
        pick = iota((cap, length), 0).astype(F32) == rank
        chosen = jnp.where(pick, 1.0, 0.0).astype(BF16)
        taken = dot_nn(chosen, jnp.concatenate([self.nm[p], self.upstream[p]], axis=1))
        gate_col = jnp.sum(jnp.where(pick, gate_row, 0.0), axis=1, keepdims=True)
        x = taken[:, :width].astype(BF16)
        g = taken[:, width:]
        self.x_s[here, :] = x
        grad_out = (gate_col * g).astype(BF16)
        self.go_s[here, :] = grad_out
        gate = dot_nn(x, self.inner_w[:, :hidden_width])
        up = dot_nn(x, self.inner_w[:, hidden_width:])
        sigma = 1.0 / (1.0 + jnp.exp(-gate))
        active = gate * sigma
        hidden = (active * up).astype(BF16)
        self.hid_s[here, :] = hidden
        result = dot_nn(hidden, self.down_w[...]).astype(BF16).astype(F32)
        spot = pl.ds(pl.multiple_of(expert * cap, cap), cap)
        self.y_s[p, spot, :width] = (gate_col * result).astype(BF16)
        grad_gate = jnp.sum(g * result, axis=1, keepdims=True)
        self.gg_s[p, pl.ds(expert, 1), :] = jnp.sum(
            jnp.where(pick, grad_gate, 0.0), axis=0, keepdims=True
        )
        grad_hidden = dot_nt(grad_out, self.down_w[...])
        self.gb_s[here, :hidden_width] = (
            grad_hidden * up * sigma * (1.0 + gate * (1.0 - sigma))
        ).astype(BF16)
        self.gb_s[here, hidden_width:] = (grad_hidden * active).astype(BF16)
        self.y_s[p, spot, width:] = dot_nt(self.gb_s[here, :], self.inner_w[...]).astype(BF16)

    def grads(self, part):
        copies, _, width = part.shape
        hidden_width = self.hid_s.shape[1]
        deep, span = width // copies, hidden_width // copies
        for block in range(2 * hidden_width // width):
            lanes = slice(block * width, block * width + width)
            grad = dot_tn(self.x_s[...], self.gb_s[:, lanes]).astype(BF16)
            for d in range(copies):
                part[d, block * deep : block * deep + deep, :] = grad[d * deep : d * deep + deep]
        grad = dot_tn(self.hid_s[...], self.go_s[...]).astype(BF16)
        for d in range(copies):
            part[d, width:, :] = grad[d * span : d * span + span]

    def finish(self, p, router_w, mid, block_o, gmid_o, glog_o):
        cap = self.cap
        _, length, width = self.nm.shape
        experts = router_w.shape[0]
        ranks = self.rank_s[p].T
        slot = iota((length, cap), 1).astype(F32)
        pieces = [
            jnp.where(ranks[:, e : e + 1] == slot, 1.0, 0.0).astype(BF16) for e in range(experts)
        ]
        back = dot_nn(jnp.concatenate(pieces, axis=1), self.y_s[p])
        gate = self.gate_s[p]
        grad_gate = self.gg_s[p]
        mean = jnp.sum(gate * grad_gate, axis=0, keepdims=True)
        hit = self.rank_s[p] > -0.5
        grad_logits = jnp.where(hit, gate * (grad_gate - mean), 0.0).astype(BF16)
        glog_o[p] = grad_logits
        block_o[p] = (mid[p] + back[:, :width]).astype(BF16)
        gmid_o[p] = back[:, width:] + dot_tn(grad_logits, router_w[...])


def unpack(weights, inner_w, down_w):
    copies, _, width = weights.shape
    deep, span = width // copies, down_w.shape[0] // copies
    for d in range(copies):
        for block in range(inner_w.shape[1] // width):
            inner_w[d * deep : d * deep + deep, block * width : block * width + width] = weights[
                d, block * deep : block * deep + deep, :
            ]
        down_w[d * span : d * span + span, :] = weights[d, width:, :]


def forward_kernel(
    line, cap,
    shard, patches, upstream, items, ids, qkv_w, proj_w, router_w, gains, table,
    full, kept_o, mixed_o, probs_o, att_o, mid_o, nm_o, block_o, gmid_o, glog_o,
    qkv_s, proj_s, mixed_s, probs_s, att_s, mid_s, nm_s, wbuf, pbuf,
    rank_s, gate_s, gg_s, x_s, hid_s, go_s, gb_s, y_s, inner_s, down_s,
    sums, core_in, diag_in, side_in,
    send_sem, recv_sem, own_sem, save_sem, fetch_sem, keep_sem,
    core_send, core_sem, diag_send, diag_sem, side_send, side_sem, credit_sem,
):
    packs = patches.shape[0]
    experts = router_w.shape[0]
    place = Place(line)
    place.greet()
    gather = Gather(place, shard, full, send_sem, recv_sem, own_sem)
    gather.start()
    qkv_s[...] = qkv_w[...].astype(BF16)
    proj_s[...] = proj_w[...].astype(BF16)
    work = Experts(
        (nm_s, upstream, rank_s, gate_s, gg_s, x_s, hid_s, go_s, gb_s, y_s, inner_s, down_s), cap
    )
    saves = ((mixed_s, mixed_o), (probs_s, probs_o), (att_s, att_o), (mid_s, mid_o), (nm_s, nm_o))

    def save(n, p):
        source, target = saves[n]
        return pltpu.make_async_copy(
            source.at[lax.rem(p, source.shape[0])], target.at[p], save_sem.at[n, p]
        )

    def pack(p, carry):
        pl.when(p >= 2)(lambda: save(0, p - 2).wait())
        attend_pack(p, patches, items, gains, table, qkv_s, proj_s, mixed_s, probs_s, att_s, mid_s, nm_s)
        for n in range(len(saves)):
            save(n, p).start()
        work.prepare(p, ids, router_w)
        for k in range(1, line):

            def relay(k=k):
                gather.column(k)
                gather.square(k - 1)

            pl.when(p == min(k - 1, packs - 1))(relay)
        return carry

    lax.fori_loop(0, packs, pack, 0)

    def near(i):
        return int(i < line) if isinstance(i, int) else (i < line).astype(jnp.int32)

    def number(i):
        level = place.by_distance(near(i) * i + (1 - near(i)) * (2 * line - 1 - i))
        side = near(i) * place.y + (1 - near(i)) * (1 - place.y)
        return level, 2 * level + side

    def fetch(i):
        return pltpu.make_async_copy(full.at[number(i)[1]], wbuf.at[lax.rem(i, 2)], fetch_sem.at[lax.rem(i, 2)])

    def arrive(i):
        level = number(i)[0]

        def close():
            gather.partner(0, 0, level)
            gather.partner(1, 0, level)

        def far():
            gather.partner(0, 1, level)
            gather.partner(1, 1, level)

        if isinstance(i, int):
            (close if i < line else far)()
        else:
            pl.when(i < line)(close)
            pl.when(i >= line)(far)

    def piece(q, flip_core):
        return place.device(q, 0, flip_core)[0]

    def swap(i, q):
        slot = lax.rem(i, 2)
        return remote(
            pbuf.at[slot, piece(q, 1)], core_in.at[slot, q], core_send.at[slot, q], core_sem.at[slot, q],
            place.device(0, 0, 1),
        )

    def across(n):
        level = number(line + n)[0]
        return remote(
            sums.at[ACROSS, level], diag_in.at[n], diag_send.at[n], diag_sem.at[n], place.device(1)
        )

    def aside(level):
        return remote(
            sums.at[OVER_X, level], side_in.at[level], side_send.at[level], side_sem.at[level],
            place.device(1),
        )

    def keep(which, group, level):
        return pltpu.make_async_copy(sums.at[group, level], kept_o.at[which, level], keep_sem.at[which, level])

    def merge(i):
        slot = lax.rem(i, 2)
        level = number(i)[0]
        group = 2 * (1 - near(i))
        for q in range(2):
            swap(i, q).wait_recv()
            total = pbuf[slot, piece(q, 0)].astype(F32) + core_in[slot, q].astype(F32)
            sums[group + q, level] = total.astype(BF16)
        pl.semaphore_signal(credit_sem, inc=1, device_id=place.device(0, 0, 1), device_id_type=MESH_ID)
        pl.when(i < line)(lambda: aside(level).start())
        for n in range(EARLY):
            pl.when(i == line + n)(lambda n=n: across(n).start())

        def put_away():
            keep(1, OVER_Y, level).start()
            keep(2, ACROSS, level).start()

        pl.when(i >= line + EARLY)(put_away)

    gather.own.wait()
    arrive(0)
    fetch(0).start()

    def one(i, carry):
        fetch(i).wait()
        unpack(wbuf.at[lax.rem(i, 2)], inner_s, down_s)
        expert = number(i)[1]

        def rows(p, inner_carry):
            work.rows(p, expert)
            pl.when(jnp.logical_and(p == 0, i >= 1))(lambda: merge(i - 1))
            return inner_carry

        lax.fori_loop(0, packs, rows, 0)

        def corners(found):
            for k in found:
                gather.corner(k)

        pl.when(i == line - 3)(lambda: gather.square(line - 1))
        pl.when(i == line - 2)(lambda: corners(range(line - 1)))
        pl.when(i == line - 1)(lambda: corners((line - 1,)))

        def ahead():
            arrive(i + 1)
            fetch(i + 1).start()

        pl.when(i + 1 < experts)(ahead)

        def free():
            pl.semaphore_wait(credit_sem, 1)
            for q in range(2):
                swap(i, q).wait_send()

        pl.when(i >= 2)(free)
        work.grads(pbuf.at[lax.rem(i, 2)])
        for q in range(2):
            swap(i, q).start()
        return carry

    lax.fori_loop(0, experts, one, 0)

    def last(i, carry):
        merge(i)
        return carry

    lax.fori_loop(experts - 1, experts, last, 0)

    def finish(p, carry):
        work.finish(p, router_w, mid_s, block_o, gmid_o, glog_o)
        return carry

    lax.fori_loop(0, packs, finish, 0)

    def settle(level, carry):
        aside(level).wait_recv()
        sums[OWN, level] = (sums[OWN, level].astype(F32) + side_in[level].astype(F32)).astype(BF16)
        keep(0, OWN, level).start()
        return carry

    lax.fori_loop(0, line, settle, 0)
    for n in range(EARLY):
        level = number(line + n)[0]
        across(n).wait_recv()
        sums[OVER_Y, level] = (sums[OVER_Y, level].astype(F32) + diag_in[n].astype(F32)).astype(BF16)
        keep(1, OVER_Y, level).start()
        across(n).wait_send()

    def drain(level, carry):
        keep(0, OWN, level).wait()
        keep(1, OVER_Y, level).wait()
        aside(level).wait_send()
        return carry

    lax.fori_loop(0, line, drain, 0)
    for n in range(EARLY, line):
        keep(2, ACROSS, number(line + n)[0]).wait()
    pl.semaphore_wait(credit_sem, 2)
    for i in range(experts - 2, experts):
        for q in range(2):
            swap(i, q).wait_send()
    for n in range(len(saves)):
        for p in range(packs - 2 if n == 0 else 0, packs):
            save(n, p).wait()
    gather.wires.finish()


def run_forward(shard, patches, upstream, items, ids, qkv_w, proj_w, router_w, gains, table, hidden, slot):
    packs, length, width = patches.shape
    experts = router_w.shape[0]
    dp, ex = lax.axis_size("dp"), lax.axis_size("expert")
    line = ex // 2
    cap = 2 * length * ids.shape[1] // experts
    pairs, blocks = width // 128, length // QB
    rows = shard.shape[0]
    dma = pltpu.SemaphoreType.DMA
    here = pl.BlockSpec(memory_space=pltpu.VMEM)
    away = pl.BlockSpec(memory_space=pl.ANY)
    saved = (
        ((packs, length, 3 * width), BF16),
        ((packs, pairs, blocks, 3 * QB, 2 * QB), BF16),
        ((packs, length, width), BF16),
        ((packs, length, width), F32),
        ((packs, length, width), BF16),
    )
    shapes = (
        ((ex, dp, rows, width), BF16),
        ((3, line, rows, width), BF16),
        *saved,
        ((packs, length, width), BF16),
        ((packs, length, width), F32),
        ((packs, experts, length), BF16),
    )
    scratch = (
        ((width, 3 * width), BF16),
        ((width, width), BF16),
        ((2, length, 3 * width), BF16),
        *saved[1:],
        ((2, dp, rows, width), BF16),
        ((2, dp, rows, width), BF16),
        ((packs, experts, length), F32),
        ((packs, experts, length), F32),
        ((packs, experts, length), F32),
        ((packs * cap, width), BF16),
        ((packs * cap, hidden), BF16),
        ((packs * cap, width), BF16),
        ((packs * cap, 2 * hidden), BF16),
        ((packs, experts * cap, 2 * width), BF16),
        ((width, 2 * hidden), BF16),
        ((hidden, width), BF16),
        ((4, line, rows, width), BF16),
        ((2, 2, rows, width), BF16),
        ((EARLY, rows, width), BF16),
        ((line, rows, width), BF16),
    )
    return pl.pallas_call(
        functools.partial(forward_kernel, line, cap),
        out_shape=tuple(jax.ShapeDtypeStruct(*s) for s in shapes),
        in_specs=[here] * 10,
        out_specs=(away,) * 7 + (here,) * 3,
        scratch_shapes=[pltpu.VMEM(*s) for s in scratch]
        + [dma((24 * line,)), dma((ex, dp)), dma, dma((5, packs)), dma((2,)), dma((3, line))]
        + [dma((2, 2))] * 2 + [dma((EARLY,))] * 2 + [dma((line,))] * 2 + [pltpu.SemaphoreType.REGULAR],
        compiler_params=pltpu.CompilerParams(
            collective_id=slot, has_side_effects=True, vmem_limit_bytes=VMEM_BYTES
        ),
        name="forward",
    )(shard, patches, upstream, items, ids, qkv_w, proj_w, router_w, gains, table)


class Backward:
    def __init__(self, refs):
        (
            self.patches, self.upstream, self.items, self.gains, self.table, self.gmid, self.glog,
            self.qkv_s, self.proj_s, self.mixed, self.probs, self.mid, self.nm,
            self.patch_o, self.normed_s, self.branch_s, self.datt_s, self.dmix_s, self.dkv_s, self.small_g,
        ) = refs

    def pack(self, p):
        packs, length, width = self.patches.shape
        pairs = width // 128
        experts = self.glog.shape[1]
        gains, mixed, dkv_s = self.gains, self.mixed, self.dkv_s
        low_lane = iota((1, width), 1) % HEAD < HEAD // 2
        first_head = iota((1, 128), 1) < HEAD
        mask_a = jnp.where(first_head, 1.0, 0.0).astype(BF16)
        mask_b = jnp.where(first_head, 0.0, 1.0).astype(BF16)
        top_rows = iota((128, 1), 0) < HEAD
        rows = pl.ds(pl.multiple_of(p * length, length), length)
        source = self.patches[p].astype(F32)
        gain0, gain1 = gains[0:1, :], gains[1:2, :]
        slot = lax.rem(p, 2)
        middle = self.mid[slot]
        inv = row_norm(middle)
        unit = middle * inv
        grad_mid = self.gmid[p]
        self.small_g[experts + 1 : experts + 2, :] += jnp.sum(grad_mid * unit, axis=0, keepdims=True)
        self.small_g[0:experts, :] += dot_nn(self.glog[p], self.nm[slot])
        grad_unit = grad_mid * gain1
        grad_middle = self.upstream[p].astype(F32) + inv * (
            grad_unit - unit * jnp.mean(grad_unit * unit, axis=1, keepdims=True)
        )
        self.patch_o[p] = grad_middle
        branch = grad_middle.astype(BF16)
        self.branch_s[rows, :] = branch
        self.datt_s[...] = dot_nt(branch, self.proj_s[...]).astype(BF16)
        dkv_s[...] = jnp.zeros(dkv_s.shape, F32)
        item_row = self.items[p].astype(F32)
        item_col, offset = positions(item_row, length)
        cos_row, sin_row = rope_rows(offset, self.table[...], length, width)
        for pair in range(pairs):
            lanes = slice(128 * pair, 128 * pair + 128)
            key_lanes = slice(width + 128 * pair, width + 128 * pair + 128)
            value_lanes = slice(2 * width + 128 * pair, 2 * width + 128 * pair + 128)
            keys_t = mixed[slot, :, key_lanes].astype(F32).T.astype(BF16)
            for block, (start, low, high) in enumerate(windows(length)):
                query = mixed[slot, start : start + QB, lanes] * 0.125
                query = jnp.concatenate([query * mask_a, query * mask_b], axis=0)
                datt = self.datt_s[start : start + QB, lanes]
                datt = jnp.concatenate([datt * mask_a, datt * mask_b], axis=0)
                prob = self.probs[slot, pair, block, : high - low]
                dprob = dot_nt(mixed[slot, low:high, value_lanes], datt)
                weight = prob.astype(F32)
                mean = jnp.sum(weight * dprob, axis=0, keepdims=True)
                dscore = (weight * (dprob - mean)).astype(BF16)
                dkv_s[low:high, key_lanes] += dot_nn(dscore, query)
                dkv_s[low:high, value_lanes] += dot_nn(prob, datt)
                dquery = dot_nn(keys_t[:, low:high], dscore)
                dquery = jnp.where(top_rows, dquery[:, :QB], dquery[:, QB:])
                dkv_s[start : start + QB, lanes] = dquery.T * 0.125
        dmix_s = self.dmix_s
        dmix_s[rows, :width] = turn(dkv_s[:, :width], cos_row, -sin_row, low_lane).astype(BF16)
        dmix_s[rows, width : 2 * width] = turn(
            dkv_s[:, width : 2 * width], cos_row, -sin_row, low_lane
        ).astype(BF16)
        dmix_s[rows, 2 * width :] = dkv_s[:, 2 * width :].astype(BF16)
        grad_normed = dot_nt(dmix_s[rows, :], self.qkv_s[...])
        inv_in = row_norm(source)
        unit_in = source * inv_in
        self.normed_s[rows, :] = (unit_in * gain0).astype(BF16)
        self.small_g[experts : experts + 1, :] += jnp.sum(grad_normed * unit_in, axis=0, keepdims=True)
        grad_unit_in = grad_normed * gain0
        self.patch_o[p] += inv_in * (
            grad_unit_in - unit_in * jnp.mean(grad_unit_in * unit_in, axis=1, keepdims=True)
        )

    def tail(self, att, tail):
        packs, length, width = self.patches.shape
        tail[...] = jnp.zeros(tail.shape, BF16)
        for block in range(4):
            if block < 3:
                grad = dot_tn(self.normed_s[...], self.dmix_s[:, block * width : block * width + width])
            else:
                flat = jnp.concatenate([att[p] for p in range(packs)], axis=0)
                grad = dot_tn(flat, self.branch_s[...])
            lay_tail(tail, block, grad.astype(BF16))
        tail[0, 0, tail.shape[2] - 16 :, :] = self.small_g[...].astype(BF16)


def tail_rows(width, devices):
    return 4 * width // devices + 16


def lay_tail(tail, block, grad):
    ex, dp, rows, width = tail.shape
    rows = rows - 16
    each = width // rows
    for piece in range(each):
        number = block * each + piece
        tail[number // dp, number % dp, :rows, :] = grad[piece * rows : piece * rows + rows]


def backward_kernel(
    line,
    kept, patches, upstream, items, qkv_w, proj_w, gains, table, gmid, glog, mixed_i, probs_i, att_i, mid_i, nm_i,
    patch_o, grad_o, tail_o,
    qkv_s, proj_s, mixed, probs, att, mid, nm,
    normed_s, branch_s, datt_s, dmix_s, dkv_s, small_g, tail, tail_sum, tail_low,
    owns, sides, diag_in, side_in, line_in,
    tsums, tcore_in, tdiag_in, tside_in, tline_in,
    load_sem, own_sem, diag_send, diag_sem, side_send, side_sem, line_send, line_sem,
    tsend_sem, tcore_sem, tdiag_sem, tside_sem, tline_sem, tcopy_sem,
    gsend_sem, grecv_sem, gown_sem,
):
    packs = patches.shape[0]
    place = Place(line)
    place.greet()
    reduce = Close(
        place, kept, owns, sides, diag_in, side_in, line_in, own_sem,
        (diag_send, diag_sem, side_send, side_sem, line_send, line_sem),
    )
    small = Reduce(
        place, tail, tsums, tcore_in, tdiag_in, tside_in, tline_in,
        tsend_sem, (tcore_sem, tdiag_sem, tside_sem, tline_sem), tcopy_sem,
    )
    order = list(range(line - 1, -1, -1))
    reduce.start()
    loads = ((mixed_i, mixed), (mid_i, mid), (nm_i, nm), (probs_i, probs), (att_i, att))

    def load(n, p):
        source, target = loads[n]
        return pltpu.make_async_copy(
            source.at[p], target.at[lax.rem(p, target.shape[0])], load_sem.at[n, p]
        )

    for p in range(packs):
        for n in range(len(loads)):
            if p < loads[n][1].shape[0]:
                load(n, p).start()
    qkv_s[...] = qkv_w[...].astype(BF16)
    proj_s[...] = proj_w[...].astype(BF16)
    small_g[...] = jnp.zeros(small_g.shape, F32)
    work = Backward((
        patches, upstream, items, gains, table, gmid, glog,
        qkv_s, proj_s, mixed, probs, mid, nm,
        patch_o, normed_s, branch_s, datt_s, dmix_s, dkv_s, small_g,
    ))
    def pack(p, carry):
        for n in range(len(loads)):
            load(n, p).wait()
        work.pack(p)

        def ahead():
            for n in range(len(loads) - 1):
                load(n, p + 2).start()

        pl.when(p + 2 < packs)(ahead)

        def advance(n):
            if n + 1 < line:
                reduce.send_side(n + 1)
            reduce.send_line(n)

        for n in range(min(packs, line - 1)):
            pl.when(p == n)(lambda n=n: advance(n))
        return carry

    lax.fori_loop(0, packs, pack, 0)
    work.tail(att, tail)
    for group in (ACROSS, OVER_X, OVER_Y, OWN):
        for away in order:
            small.share(group, away)
    for away in order:
        small.merge(ACROSS, away)
        small.send_across(away)
    for group in (OVER_X, OVER_Y, OWN):
        for away in order:
            small.merge(group, away)
    for away in order:
        small.send_side(away)
    for away in order[:-1]:
        small.send_line(away)
    small.finish(tail_sum)
    tail_low[...] = tail_sum[...].astype(BF16)
    gather = Gather(place, tail_low, tail_o, gsend_sem, grecv_sem, gown_sem)
    gather.start()
    reduce.finish(grad_o)
    for away in range(1, line):
        gather.column(away)
        gather.square(away - 1)
    gather.square(line - 1)
    for away in range(line):
        gather.corner(away)
    for flip_x in range(2):
        for flip_y in range(2):
            for away in range(line):
                for dist, level, test, way in place.levels():
                    if dist == away:
                        only(test, lambda: gather.partner(flip_x, flip_y, level))
    gather.own.wait()
    gather.wires.finish()


def run_backward(
    kept, patches, upstream, items, qkv_w, proj_w, gains, table, gmid, glog, mixed, probs, att, mid, nm, slot
):
    packs, length, width = patches.shape
    _, line, rows, _ = kept.shape
    dp, ex = lax.axis_size("dp"), lax.axis_size("expert")
    few = tail_rows(width, ex * dp)
    dma = pltpu.SemaphoreType.DMA
    here = pl.BlockSpec(memory_space=pltpu.VMEM)
    away = pl.BlockSpec(memory_space=pl.ANY)
    shapes = (
        ((packs, length, width), F32),
        ((rows, width), F32),
        ((ex, dp, few, width), BF16),
    )
    slabs = lambda r: tuple(
        (dims + (r, width), BF16) for dims in ((4, line), (4, line), (line,), (2, line), (2, line))
    )
    scratch = (
        ((width, 3 * width), BF16),
        ((width, width), BF16),
        ((2,) + mixed.shape[1:], BF16),
        ((2,) + probs.shape[1:], BF16),
        (att.shape, BF16),
        ((2,) + mid.shape[1:], F32),
        ((2,) + nm.shape[1:], BF16),
        ((packs * length, width), BF16),
        ((packs * length, width), BF16),
        ((length, width), BF16),
        ((packs * length, 3 * width), BF16),
        ((length, 3 * width), F32),
        ((16, width), F32),
        ((ex, dp, few, width), BF16),
        ((few, width), F32),
        ((few, width), BF16),
        *([((line, rows, width), BF16)] * 5),
        *slabs(few),
    )
    reduce_sems = [dma((20 * line,)), dma((4, line)), dma((line,)), dma((2, line)), dma((2, line)), dma((4, line))]
    return pl.pallas_call(
        functools.partial(backward_kernel, line),
        out_shape=tuple(jax.ShapeDtypeStruct(*s) for s in shapes),
        in_specs=[away] + [here] * 9 + [away] * 5,
        out_specs=(here, here, here),
        scratch_shapes=[pltpu.VMEM(*s) for s in scratch]
        + [dma((5, packs)), dma((2, line))] + [dma((line,))] * 6 + reduce_sems
        + [dma((24 * line,)), dma((ex, dp)), dma],
        compiler_params=pltpu.CompilerParams(
            collective_id=slot, has_side_effects=True, vmem_limit_bytes=VMEM_BYTES
        ),
        name="backward",
    )(kept, patches, upstream, items, qkv_w, proj_w, gains, table, gmid, glog, mixed, probs, att, mid, nm)


def update_kernel(
    tail, inner_g, down_g,
    qkv_w, qkv_f, qkv_s, proj_w, proj_f, proj_s, router_w, router_f, router_s,
    gains_w, gains_f, gains_s, inner_w, inner_f, inner_s, down_w, down_f, down_s,
    qkv_wo, qkv_fo, qkv_so, proj_wo, proj_fo, proj_so, router_wo, router_fo, router_so,
    gains_wo, gains_fo, gains_so, inner_wo, inner_fo, inner_so, down_wo, down_fo, down_so,
):
    step = pl.program_id(0)
    ex, dp, few, width = tail.shape
    rows = few - 16
    experts = router_w.shape[1]
    attn = tail[:, :, :rows, :].reshape(ex * dp * rows, width).astype(F32)

    def write(outs, values):
        for out, value in zip(outs, values):
            out[...] = value

    def qkv():
        write((qkv_wo, qkv_fo, qkv_so), adamw(qkv_w[...], qkv_f[...], qkv_s[...], attn, 0.1, 0.1))

    def proj():
        write((proj_wo, proj_fo, proj_so), adamw(proj_w[...], proj_f[...], proj_s[...], attn, 0.4, 0.1))

    def rest():
        small = tail[0, 0, rows:, :].astype(F32)
        router_g = small.T[:, :experts]
        gains_g = small[experts : experts + 2]
        write(
            (router_wo, router_fo, router_so),
            adamw(router_w[...], router_f[...], router_s[...], router_g, 0.07, 0.1),
        )
        write(
            (gains_wo, gains_fo, gains_so),
            adamw(gains_w[...], gains_f[...], gains_s[...], gains_g, 0.4, 0.0),
        )

    pl.when(step < 3)(qkv)
    pl.when(step == 3)(proj)
    pl.when(step == 0)(rest)
    write(
        (inner_wo, inner_fo, inner_so),
        adamw(inner_w[...], inner_f[...], inner_s[...], inner_g[...], 0.1, 0.1),
    )
    write((down_wo, down_fo, down_so), adamw(down_w[...], down_f[...], down_s[...], down_g[...], 0.15, 0.1))


def run_update(tail, grad, weights):
    ex, dp, few, width = tail.shape
    qkv, router, inner, down = weights[0], weights[6], weights[12], weights[15]
    deep, span = inner.shape[0], down.shape[0] // 4
    of_qkv = pl.BlockSpec((width, width), lambda j: (0, jnp.minimum(j, 2)))
    of_proj = pl.BlockSpec((width, width), lambda j: (0, 0))
    of_router = pl.BlockSpec(router.shape, lambda j: (0, 0))
    of_gains = pl.BlockSpec((2, width), lambda j: (0, 0))
    of_inner = pl.BlockSpec((deep, width), lambda j: (0, j))
    of_down = pl.BlockSpec((span, width), lambda j: (j, 0))
    specs = []
    for spec in (of_qkv, of_proj, of_router, of_gains, of_inner, of_down):
        specs += [spec] * 3
    first_down = 4 * deep // span
    return pl.pallas_call(
        update_kernel,
        out_shape=tuple(jax.ShapeDtypeStruct(w.shape, F32) for w in weights),
        grid=(4,),
        in_specs=[
            pl.BlockSpec((ex // 4, dp, few, width), lambda j: (j, 0, 0, 0)),
            pl.BlockSpec((deep, width), lambda j: (j, 0)),
            pl.BlockSpec((span, width), lambda j: (first_down + j, 0)),
        ] + specs,
        out_specs=tuple(specs),
        compiler_params=pltpu.CompilerParams(vmem_limit_bytes=VMEM_BYTES),
        name="update",
    )(tail, grad, grad, *weights)


def fast(
    patches, out_grad, item_ids, expert_ids,
    qkv_master, qkv_first, qkv_second,
    proj_master, proj_first, proj_second,
    router_master, router_first, router_second,
    gains_master, gains_first, gains_second,
    inner_master, inner_first, inner_second,
    down_master, down_first, down_second,
):
    width = patches.shape[2]
    experts = router_master.shape[1]
    hidden = down_master.shape[1] * lax.axis_size("dp")
    deep = inner_master.shape[1]
    blocks = inner_master.shape[2] // width
    shard = jnp.concatenate(
        [
            jnp.swapaxes(inner_master[0].reshape(deep, blocks, width), 0, 1).reshape(blocks * deep, width),
            down_master[0],
        ],
        axis=0,
    ).astype(BF16)
    router_w = router_master.T.astype(BF16)
    ids = jnp.swapaxes(expert_ids, 1, 2)
    table = jnp.asarray(rope_table(QB))
    full, kept, mixed, probs, att, mid, nm, block_out, gmid, glog = run_forward(
        shard, patches, out_grad, item_ids, ids, qkv_master, proj_master, router_w, gains_master, table, hidden, 0
    )
    patch_grad, grad, tail = run_backward(
        kept, patches, out_grad, item_ids, qkv_master, proj_master, gains_master, table,
        gmid, glog, mixed, probs, att, mid, nm, 1,
    )
    weights = (
        qkv_master, qkv_first, qkv_second,
        proj_master, proj_first, proj_second,
        router_master, router_first, router_second,
        gains_master, gains_first, gains_second,
        inner_master[0], inner_first[0], inner_second[0],
        down_master[0], down_first[0], down_second[0],
    )
    new = run_update(tail, grad, weights)
    return (block_out, patch_grad, *new[:12], *(value[None] for value in new[12:]))


GATHER_LIMIT = 16 * 1024 * 1024


def step(*args):
    inner_master, down_master = args[16], args[19]
    experts = inner_master.shape[0] * lax.axis_size("expert")
    entries = inner_master.shape[1] * inner_master.shape[2] + down_master.shape[1] * down_master.shape[2]
    weight_bytes = 2 * experts * entries * lax.axis_size("dp")
    square = lax.axis_size("dp") == 4 and inner_master.shape[0] == 1 and lax.axis_size("expert") == experts
    return (fast if square and weight_bytes <= GATHER_LIMIT else local)(*args)


def solution(mesh):
    in_specs = (
        P(None, ("dp", "expert"), None),
        P(None, ("dp", "expert"), None),
        P(None, ("dp", "expert"), None),
        P(None, ("dp", "expert"), None),
        P(),
        P(),
        P(),
        P(),
        P(),
        P(),
        P(),
        P(),
        P(),
        P(),
        P(),
        P(),
        P("expert", "dp", None),
        P("expert", "dp", None),
        P("expert", "dp", None),
        P("expert", "dp", None),
        P("expert", "dp", None),
        P("expert", "dp", None),
    )
    out_specs = (
        P(None, ("dp", "expert"), None),
        P(None, ("dp", "expert"), None),
        P(),
        P(),
        P(),
        P(),
        P(),
        P(),
        P(),
        P(),
        P(),
        P(),
        P(),
        P(),
        P("expert", "dp", None),
        P("expert", "dp", None),
        P("expert", "dp", None),
        P("expert", "dp", None),
        P("expert", "dp", None),
        P("expert", "dp", None),
    )
    return jax.shard_map(step, mesh=mesh, in_specs=in_specs, out_specs=out_specs, check_vma=False)
```

profile of v0, /device:TPU:0, one launch (start us, length us, event | category | flops | bytes accessed | tf_op | source)
XLA Modules:
  0.0 245.3 jit_solution(8867675034956527578)
XLA Ops:
  0.7 0.0 copy-start.1
  0.7 0.0 copy-start.2
  0.7 1.1 convert.9
  1.8 0.1 reshape_squeeze.4
  1.9 0.0 copy-done.1
  2.0 0.8 pad_maximum_fusion.shard
  2.8 0.0 copy-done.2
  2.8 0.6 convert_bitcast_fusion.router_w
  3.4 132.8 %forward.1 = (bf16[8,4,576,384]{3,2,1,0:T(8,128)(2,1)}, bf16[3,4,576,384]{3,2,1,0:T(8,128)(2,1)}, bf16[3,512,1152]{2,1,0:T(8,128)(2,1)}, bf16[3,3,4,384,256]{4,3...) custom-call(bf16[576,384]{1,0:T(8,128)(2,1)} %pad_maximum_fusion.sha, ...), custom_call_target="tpu_custom_call" | custom-call | tf_op jit(solution)/shard_map/forward/pallas_call | solution.py:1220
  136.2 0.0 copy-start.3
  136.2 0.0 copy-start.4
  136.2 86.9 %backward.1 = (f32[3,512,384]{2,1,0:T(8,128)}, f32[576,384]{1,0:T(8,128)}, bf16[8,4,64,384]{3,2,1,0:T(8,128)(2,1)}) custom-call(bf16[3,4,576,384]{3,2,1,0:T(8,128)(2,1)} %get-tuple-element.51.kept, bf16[3,512,384]{2,1,0:T(8,128)(2,1)} %patches.3, bf16[3,512,384]{2,1,0:T(8,128)(2,1)} %upstream.3, s32[3,1,512]{2,1,0:T(1,128)} %items.3, f32[384,1152]{1,0:T(8,128)} %qkv_w.5, ...), custom_call_target="tpu_custom_call" | custom-call | tf_op jit(solution)/shard_map/backward/pallas_call | solution.py:1477
  223.1 0.8 copy.44.router_w
  223.9 0.0 copy-done.3
  223.9 0.8 copy.45.router_f
  224.7 0.0 copy-done.4
  224.7 0.8 copy.46.router_s
  225.5 11.0 %update.1 = (f32[384,1152]{1,0:T(8,128)}, f32[384,1152]{1,0:T(8,128)}, f32[384,1152]{1,0:T(8,128)}, f32[384,384]{1,0:T(8,128)}, f32[384,384]{1,0:T(8,128)}, /*in...) custom-call(bf16[8,4,64,384]{3,2,1,0:T(8,128)(2,1)} %get-tuple-eleme, ...), custom_call_target="tpu_custom_call" | custom-call | tf_op jit(solution)/shard_map/update/pallas_call | solution.py:1552
  236.5 1.8 copy.47
  238.3 1.6 copy.48
  239.9 1.6 copy.49
  241.5 2.4 copy.52
  243.9 0.0 copy-done
  243.9 1.4 copy.53
  (3 shorter events, 0.1 us)
Async XLA Ops:
  0.7 1.3 copy-start.1
  0.7 2.1 copy-start.2
  136.2 87.7 %copy-start.3 = (f32[384,8]{0,1:T(8,128)S(1)}, f32[384,8]{0,1:T(8,128)}, u32[]{:S(2)}) copy-start(f32[384,8]{0,1:T(8,128)} %param.34) | copy-start | bytes 36868
  136.2 88.5 %copy-start.4 = (f32[384,8]{0,1:T(8,128)S(1)}, f32[384,8]{0,1:T(8,128)}, u32[]{:S(2)}) copy-start(f32[384,8]{0,1:T(8,128)} %param.35) | copy-start | bytes 36868
  236.5 7.4 %copy-start = (f32[3,512,384]{2,1,0:T(8,128)S(1)}, f32[3,512,384]{2,1,0:T(8,128)}, u32[]{:S(2)}) copy-start(f32[3,512,384]{2,1,0:T(8,128)} %get-tuple-element.121) | copy-start | bytes 7077892
where the time goes:
time: 246 us; the launch traced here: 245 us
  Pallas kernels  231 us (94%)
  local copies, waits for them, and re-layouts  11.4 us (5%)
  other arithmetic  2.56 us (1%)
    pallas_call x1, Pallas kernels, run_forward(): pl.pallas_call(functools.partial(forward_kernel, line, cap), out_shape=tu...  133 us
    pallas_call x1, Pallas kernels, run_backward(): pl.pallas_call(functools.partial(backward_kernel, line), out_shape=tuple(...  86.9 us
    unnamed x18, local copies, waits for them, and re-layouts  11.3 us
    pallas_call x1, Pallas kernels, run_update(): pl.pallas_call(update_kernel, out_shape=tuple((jax.ShapeDtypeStruct(w.sha...  11 us

commit v1 on v0

--- a/solution.py
+++ b/solution.py
@@ -434,11 +434,11 @@
         def signal(device):
             pl.semaphore_signal(barrier, inc=1, device_id=device, device_id_type=MESH_ID)
 
-        for device in (self.device(1), self.device(0, 1), self.device(0, 0, 1)):
+        for device in (self.device(1), self.device(0, 1), self.device(1, 1), self.device(0, 0, 1)):
             signal(device)
         for step in range(1, self.line):
             signal(self.device(z=lax.rem(self.z + step, self.line)))
-        pl.semaphore_wait(barrier, self.line + 2)
+        pl.semaphore_wait(barrier, self.line + 3)
 
 
 def both(*tests):
@@ -586,147 +586,7 @@
 
 
 OWN, OVER_X, OVER_Y, ACROSS = 0, 1, 2, 3
-FLIPS = ((0, 0), (1, 0), (0, 1), (1, 1))
-
-
-class Reduce:
-    def __init__(self, place, part, sums, core_in, diag_in, side_in, line_in, send_sem, recv, copy_sem):
-        self.place, self.part, self.sums = place, part, sums
-        self.core_in, self.diag_in, self.side_in, self.line_in = core_in, diag_in, side_in, line_in
-        self.core_sem, self.diag_sem, self.side_sem, self.line_sem = recv
-        self.copy_sem = copy_sem
-        self.wires = Wires(send_sem, core_in.at[0, 0])
-
-    def shard(self, group, level, flip_core=0):
-        device = self.place.device(*FLIPS[group], flip_core, z=level)
-        return self.part.at[device[1], device[0]]
-
-    def pick(self, away):
-        return [(level, test, way) for dist, level, test, way in self.place.levels() if dist == away]
-
-    def share(self, group, away):
-        for level, test, way in self.pick(away):
-            load = pltpu.make_async_copy(
-                self.shard(group, level), self.sums.at[group, level], self.copy_sem.at[group, level]
-            )
-            only(test, load.start)
-            self.wires.send(
-                self.shard(group, level, 1),
-                self.core_in.at[group, level],
-                self.core_sem.at[group, level],
-                self.place.device(0, 0, 1),
-                test,
-            )
-
-    def add(self, group, level, value):
-        self.sums[group, level] = (self.sums[group, level].astype(F32) + value.astype(F32)).astype(BF16)
-
-    def merge(self, group, away):
-        place = self.place
-        for level, test, way in self.pick(away):
-
-            def body(level=level):
-                pltpu.make_async_copy(
-                    self.shard(group, level), self.sums.at[group, level], self.copy_sem.at[group, level]
-                ).wait()
-                self.wires.arrived(
-                    self.core_in.at[group, level],
-                    self.core_sem.at[group, level],
-                    place.device(0, 0, 1),
-                )
-                self.add(group, level, self.core_in[group, level])
-
-            only(test, body)
-
-    def send_across(self, away):
-        place = self.place
-        side = OVER_Y if away % 2 == 0 else OVER_X
-        for level, test, way in self.pick(away):
-            self.wires.send(
-                self.sums.at[ACROSS, level],
-                self.diag_in.at[level],
-                self.diag_sem.at[level],
-                place.device(*FLIPS[side]),
-                test,
-            )
-
-    def send_side(self, away):
-        place = self.place
-        group = OVER_X if away % 2 == 0 else OVER_Y
-        for level, test, way in self.pick(away):
-
-            def body(level=level):
-                self.wires.arrived(self.diag_in.at[level], self.diag_sem.at[level], place.device(1))
-                self.add(group, level, self.diag_in[level])
-
-            only(test, body)
-            for side in (OVER_X, OVER_Y):
-                self.wires.send(
-                    self.sums.at[side, level],
-                    self.side_in.at[side - 1, level],
-                    self.side_sem.at[side - 1, level],
-                    place.device(*FLIPS[side]),
-                    test,
-                )
-
-    def collect(self, level, test):
-        place = self.place
-
-        def body():
-            total = self.sums[OWN, level].astype(F32)
-            for side in range(2):
-                self.wires.arrived(
-                    self.side_in.at[side, level], self.side_sem.at[side, level], place.device(1)
-                )
-                total = total + self.side_in[side, level].astype(F32)
-            self.sums[OWN, level] = total.astype(BF16)
-
-        only(test, body)
-
-    def send_line(self, away):
-        place = self.place
-        for level, test, way in self.pick(away):
-            self.collect(level, test)
-            lane = 0 if way < 0 else 1
-
-            def body(level=level, lane=lane):
-                self.wires.arrived(
-                    self.line_in.at[lane, level], self.line_sem.at[lane, level], place.device(1)
-                )
-                self.add(OWN, level, self.line_in[lane, level])
-
-            only(both(test, place.up if way < 0 else place.down), body)
-            self.wires.send(
-                self.sums.at[OWN, level],
-                self.line_in.at[lane, level],
-                self.line_sem.at[lane, level],
-                place.device(z=place.z + way),
-                test,
-            )
-
-    def finish(self, out):
-        place = self.place
-        level = place.z
-        total = self.sums[OWN, level].astype(F32)
-        for side in range(2):
-            self.wires.arrived(
-                self.side_in.at[side, level], self.side_sem.at[side, level], place.device(1)
-            )
-            total = total + self.side_in[side, level].astype(F32)
-        out[...] = total
-        for way, far in ((0, place.up), (1, place.down)):
-
-            def body(way=way):
-                self.wires.arrived(
-                    self.line_in.at[way, level], self.line_sem.at[way, level], place.device(1)
-                )
-                out[...] += self.line_in[way, level].astype(F32)
-
-            only(far, body)
-        self.wires.finish()
-
-
-EARLY = 1
+EARLY = 2
 
 
 class Close:
@@ -756,7 +616,7 @@
         source = self.kept.at[1, level] if slot < EARLY else self.sides.at[slot]
         return remote(
             source, self.side_in.at[slot], self.side_send.at[slot], self.side_sem.at[slot],
-            self.place.device(0, 1),
+            self.place.device(1) if slot == 0 else self.place.device(0, 1),
         )
 
     def along(self, slot):
@@ -804,6 +664,129 @@
                 self.across(slot).wait_send()
             if slot < last:
                 self.along(slot).wait_send()
+
+
+class Small:
+    def __init__(self, place, part, low, out, sums, core_in, square_in, line_in, sems):
+        self.place, self.part, self.low, self.out = place, part, low, out
+        self.sums, self.core_in, self.square_in, self.line_in = sums, core_in, square_in, line_in
+        (
+            self.core_send, self.core_sem, self.square_send, self.square_sem, self.line_send, self.line_sem,
+            self.up_send, self.up_sem, self.back_send, self.back_sem, self.last_send, self.last_sem,
+        ) = sems
+
+    def lane(self, group, flip_core=0):
+        place = self.place
+        x = 1 - place.x if group in (OVER_X, ACROSS) else place.x
+        y = 1 - place.y if group in (OVER_Y, ACROSS) else place.y
+        core = 1 - place.core if flip_core else place.core
+        return y, 2 * x + core
+
+    def to(self, group):
+        return self.place.device(int(group in (OVER_X, ACROSS)), int(group in (OVER_Y, ACROSS)))
+
+    def core(self, group):
+        y, d = self.lane(group, 1)
+        return remote(
+            self.part.at[y, d], self.core_in.at[group], self.core_send.at[group], self.core_sem.at[group],
+            self.place.device(0, 0, 1),
+        )
+
+    def over(self, group):
+        return remote(
+            self.sums.at[group], self.square_in.at[group - 1], self.square_send.at[group - 1],
+            self.square_sem.at[group - 1], self.to(group),
+        )
+
+    def along(self, z):
+        return remote(
+            self.sums.at[OWN, z], self.line_in.at[self.place.z], self.line_send.at[z],
+            self.line_sem.at[self.place.z], self.place.device(z=z),
+        )
+
+    def landed(self, z):
+        return remote(
+            self.sums.at[OWN, z], self.line_in.at[z], self.line_send.at[z], self.line_sem.at[z],
+            self.place.device(z=z),
+        )
+
+    def up(self, z):
+        y, d = self.lane(OWN)
+        return remote(
+            self.low, self.out.at[y, d, self.place.z], self.up_send.at[z], self.up_sem.at[self.place.z],
+            self.place.device(z=z),
+        )
+
+    def risen(self, z):
+        y, d = self.lane(OWN)
+        return remote(self.low, self.out.at[y, d, z], self.up_send.at[z], self.up_sem.at[z], self.place.device(z=z))
+
+    def back(self, group):
+        y, d = self.lane(OWN)
+        return remote(
+            self.out.at[y, d], self.out.at[y, d], self.back_send.at[group - 1], self.back_sem.at[group - 1],
+            self.to(group),
+        )
+
+    def last(self, group):
+        y, d = self.lane(group)
+        return remote(
+            self.out.at[y, d], self.out.at[y, d], self.last_send.at[group], self.last_sem.at[group],
+            self.place.device(0, 0, 1),
+        )
+
+    def others(self):
+        return [lax.rem(self.place.z + step, self.place.line) for step in range(1, self.place.line)]
+
+    def start(self):
+        for group in (ACROSS, OVER_X, OVER_Y, OWN):
+            self.core(group).start()
+
+    def run(self):
+        place = self.place
+        for group in (ACROSS, OVER_X, OVER_Y, OWN):
+            self.core(group).wait_recv()
+            total = self.part[self.lane(group)].astype(F32) + self.core_in[group].astype(F32)
+            self.sums[group] = total.astype(BF16)
+            if group != OWN:
+                self.over(group).start()
+        total = self.sums[OWN].astype(F32)
+        for group in (OVER_X, OVER_Y, ACROSS):
+            self.over(group).wait_recv()
+            total = total + self.square_in[group - 1].astype(F32)
+        self.sums[OWN] = total.astype(BF16)
+        for z in self.others():
+            self.along(z).start()
+        total = self.sums[OWN, place.z].astype(F32)
+        for z in self.others():
+            self.landed(z).wait_recv()
+            total = total + self.line_in[z].astype(F32)
+        self.low[...] = total.astype(BF16)
+        for z in self.others():
+            self.up(z).start()
+        y, d = self.lane(OWN)
+        self.out[y, d, place.z] = total.astype(BF16)
+        for z in self.others():
+            self.risen(z).wait_recv()
+        for group in (ACROSS, OVER_X, OVER_Y):
+            self.back(group).start()
+        self.last(OWN).start()
+
+    def finish(self):
+        for group in (OVER_X, OVER_Y, ACROSS):
+            self.back(group).wait_recv()
+            self.last(group).start()
+        for group in (OWN, OVER_X, OVER_Y, ACROSS):
+            self.last(group).wait_recv()
+        for group in (OWN, OVER_X, OVER_Y, ACROSS):
+            self.core(group).wait_send()
+            self.last(group).wait_send()
+            if group != OWN:
+                self.over(group).wait_send()
+                self.back(group).wait_send()
+        for z in self.others():
+            self.along(z).wait_send()
+            self.up(z).wait_send()
 
 
 def copy_all(copies):
@@ -846,7 +829,7 @@
             weights = jnp.exp(scores - peak)
             total = jnp.sum(weights, axis=0, keepdims=True)
             probs = (weights * (1.0 / total)).astype(BF16)
-            probs_s[p, pair, block, : high - low] = probs
+            probs_s[slot, pair, block, : high - low] = probs
             out = dot_nn(values_t[:, low:high], probs)
             out = jnp.where(top_rows, out[:, :QB], out[:, QB:])
             att_s[p, start : start + QB, lanes] = out.T.astype(BF16)
@@ -993,7 +976,11 @@
         )
 
     def pack(p, carry):
-        pl.when(p >= 2)(lambda: save(0, p - 2).wait())
+        def reuse():
+            save(0, p - 2).wait()
+            save(1, p - 2).wait()
+
+        pl.when(p >= 2)(reuse)
         attend_pack(p, patches, items, gains, table, qkv_s, proj_s, mixed_s, probs_s, att_s, mid_s, nm_s)
         for n in range(len(saves)):
             save(n, p).start()
@@ -1002,7 +989,8 @@
 
             def relay(k=k):
                 gather.column(k)
-                gather.square(k - 1)
+                if k != 2:
+                    gather.square(k // 2)
 
             pl.when(p == min(k - 1, packs - 1))(relay)
         return carry
@@ -1050,13 +1038,14 @@
     def across(n):
         level = number(line + n)[0]
         return remote(
-            sums.at[ACROSS, level], diag_in.at[n], diag_send.at[n], diag_sem.at[n], place.device(1)
-        )
-
-    def aside(level):
+            sums.at[ACROSS, level], diag_in.at[n], diag_send.at[n], diag_sem.at[n],
+            place.device(0, 1) if n == 0 else place.device(1),
+        )
+
+    def aside(level, group=OVER_X):
         return remote(
-            sums.at[OVER_X, level], side_in.at[level], side_send.at[level], side_sem.at[level],
-            place.device(1),
+            sums.at[group, level], side_in.at[level], side_send.at[level], side_sem.at[level],
+            place.device(1) if group == OVER_X else place.device(0, 1),
         )
 
     def keep(which, group, level):
@@ -1071,9 +1060,15 @@
             total = pbuf[slot, piece(q, 0)].astype(F32) + core_in[slot, q].astype(F32)
             sums[group + q, level] = total.astype(BF16)
         pl.semaphore_signal(credit_sem, inc=1, device_id=place.device(0, 0, 1), device_id_type=MESH_ID)
-        pl.when(i < line)(lambda: aside(level).start())
+        pl.when(jnp.logical_and(i >= 2, i < line - 1))(lambda: aside(level).start())
+
+        def early(n):
+            across(n).start()
+            if n == 0:
+                aside(level, OVER_Y).start()
+
         for n in range(EARLY):
-            pl.when(i == line + n)(lambda n=n: across(n).start())
+            pl.when(i == line + n)(lambda n=n: early(n))
 
         def put_away():
             keep(1, OVER_Y, level).start()
@@ -1084,6 +1079,23 @@
     gather.own.wait()
     arrive(0)
     fetch(0).start()
+
+    def last_square():
+        gather.square(line - 1)
+        for i in range(2):
+            aside(number(i)[0]).start()
+
+    def two_corners():
+        gather.corner(0)
+        gather.corner(1)
+
+    events = (
+        (1, 0, lambda: gather.square(line - 2)),
+        (2, 0, last_square),
+        (3, 0, two_corners),
+        (3, 1, lambda: gather.corner(line - 2)),
+        (3, packs - 1, lambda: gather.corner(line - 1)),
+    )
 
     def one(i, carry):
         fetch(i).wait()
@@ -1093,17 +1105,11 @@
         def rows(p, inner_carry):
             work.rows(p, expert)
             pl.when(jnp.logical_and(p == 0, i >= 1))(lambda: merge(i - 1))
+            for slot, turn_at, event in events:
+                pl.when(jnp.logical_and(i == slot, p == turn_at))(event)
             return inner_carry
 
         lax.fori_loop(0, packs, rows, 0)
-
-        def corners(found):
-            for k in found:
-                gather.corner(k)
-
-        pl.when(i == line - 3)(lambda: gather.square(line - 1))
-        pl.when(i == line - 2)(lambda: corners(range(line - 1)))
-        pl.when(i == line - 1)(lambda: corners((line - 1,)))
 
         def ahead():
             arrive(i + 1)
@@ -1146,8 +1152,9 @@
     for n in range(EARLY):
         level = number(line + n)[0]
         across(n).wait_recv()
-        sums[OVER_Y, level] = (sums[OVER_Y, level].astype(F32) + diag_in[n].astype(F32)).astype(BF16)
-        keep(1, OVER_Y, level).start()
+        group = OVER_X if n == 0 else OVER_Y
+        sums[group, level] = (sums[group, level].astype(F32) + diag_in[n].astype(F32)).astype(BF16)
+        keep(1, group, level).start()
         across(n).wait_send()
 
     def drain(level, carry):
@@ -1164,7 +1171,7 @@
         for q in range(2):
             swap(i, q).wait_send()
     for n in range(len(saves)):
-        for p in range(packs - 2 if n == 0 else 0, packs):
+        for p in range(packs - 2 if n < 2 else 0, packs):
             save(n, p).wait()
     gather.wires.finish()
 
@@ -1199,7 +1206,8 @@
         ((width, 3 * width), BF16),
         ((width, width), BF16),
         ((2, length, 3 * width), BF16),
-        *saved[1:],
+        ((2, pairs, blocks, 3 * QB, 2 * QB), BF16),
+        *saved[2:],
         ((2, dp, rows, width), BF16),
         ((2, dp, rows, width), BF16),
         ((packs, experts, length), F32),
@@ -1240,7 +1248,7 @@
             self.patch_o, self.normed_s, self.branch_s, self.datt_s, self.dmix_s, self.dkv_s, self.small_g,
         ) = refs
 
-    def pack(self, p):
+    def pack(self, p, midway):
         packs, length, width = self.patches.shape
         pairs = width // 128
         experts = self.glog.shape[1]
@@ -1273,6 +1281,8 @@
         item_col, offset = positions(item_row, length)
         cos_row, sin_row = rope_rows(offset, self.table[...], length, width)
         for pair in range(pairs):
+            if pair == 2:
+                midway()
             lanes = slice(128 * pair, 128 * pair + 128)
             key_lanes = slice(width + 128 * pair, width + 128 * pair + 128)
             value_lanes = slice(2 * width + 128 * pair, 2 * width + 128 * pair + 128)
@@ -1318,7 +1328,7 @@
                 flat = jnp.concatenate([att[p] for p in range(packs)], axis=0)
                 grad = dot_tn(flat, self.branch_s[...])
             lay_tail(tail, block, grad.astype(BF16))
-        tail[0, 0, tail.shape[2] - 16 :, :] = self.small_g[...].astype(BF16)
+        tail[0, 0, 0, tail.shape[3] - 16 :, :] = self.small_g[...].astype(BF16)
 
 
 def tail_rows(width, devices):
@@ -1326,12 +1336,13 @@
 
 
 def lay_tail(tail, block, grad):
-    ex, dp, rows, width = tail.shape
+    _, dp, line, rows, width = tail.shape
     rows = rows - 16
     each = width // rows
     for piece in range(each):
         number = block * each + piece
-        tail[number // dp, number % dp, :rows, :] = grad[piece * rows : piece * rows + rows]
+        spot = (number // (dp * line), number // line % dp, number % line)
+        tail[(*spot, slice(0, rows), slice(None))] = grad[piece * rows : piece * rows + rows]
 
 
 def backward_kernel(
@@ -1339,12 +1350,11 @@
     kept, patches, upstream, items, qkv_w, proj_w, gains, table, gmid, glog, mixed_i, probs_i, att_i, mid_i, nm_i,
     patch_o, grad_o, tail_o,
     qkv_s, proj_s, mixed, probs, att, mid, nm,
-    normed_s, branch_s, datt_s, dmix_s, dkv_s, small_g, tail, tail_sum, tail_low,
+    normed_s, branch_s, datt_s, dmix_s, dkv_s, small_g, tail, tail_low,
     owns, sides, diag_in, side_in, line_in,
-    tsums, tcore_in, tdiag_in, tside_in, tline_in,
+    tsums, tcore_in, tsquare_in, tline_in,
     load_sem, own_sem, diag_send, diag_sem, side_send, side_sem, line_send, line_sem,
-    tsend_sem, tcore_sem, tdiag_sem, tside_sem, tline_sem, tcopy_sem,
-    gsend_sem, grecv_sem, gown_sem,
+    *small_sems,
 ):
     packs = patches.shape[0]
     place = Place(line)
@@ -1353,11 +1363,7 @@
         place, kept, owns, sides, diag_in, side_in, line_in, own_sem,
         (diag_send, diag_sem, side_send, side_sem, line_send, line_sem),
     )
-    small = Reduce(
-        place, tail, tsums, tcore_in, tdiag_in, tside_in, tline_in,
-        tsend_sem, (tcore_sem, tdiag_sem, tside_sem, tline_sem), tcopy_sem,
-    )
-    order = list(range(line - 1, -1, -1))
+    small = Small(place, tail, tail_low, tail_o, tsums, tcore_in, tsquare_in, tline_in, small_sems)
     reduce.start()
     loads = ((mixed_i, mixed), (mid_i, mid), (nm_i, nm), (probs_i, probs), (att_i, att))
 
@@ -1382,7 +1388,17 @@
     def pack(p, carry):
         for n in range(len(loads)):
             load(n, p).wait()
-        work.pack(p)
+
+        def midway():
+            pl.when(p == 1)(lambda: reduce.send_side(2))
+
+            def later():
+                reduce.send_side(3)
+                reduce.send_line(2)
+
+            pl.when(p == packs - 1)(later)
+
+        work.pack(p, midway)
 
         def ahead():
             for n in range(len(loads) - 1):
@@ -1390,49 +1406,19 @@
 
         pl.when(p + 2 < packs)(ahead)
 
-        def advance(n):
-            if n + 1 < line:
-                reduce.send_side(n + 1)
-            reduce.send_line(n)
-
-        for n in range(min(packs, line - 1)):
-            pl.when(p == n)(lambda n=n: advance(n))
+        def first():
+            reduce.send_line(0)
+            reduce.send_line(1)
+
+        pl.when(p == 0)(first)
         return carry
 
     lax.fori_loop(0, packs, pack, 0)
     work.tail(att, tail)
-    for group in (ACROSS, OVER_X, OVER_Y, OWN):
-        for away in order:
-            small.share(group, away)
-    for away in order:
-        small.merge(ACROSS, away)
-        small.send_across(away)
-    for group in (OVER_X, OVER_Y, OWN):
-        for away in order:
-            small.merge(group, away)
-    for away in order:
-        small.send_side(away)
-    for away in order[:-1]:
-        small.send_line(away)
-    small.finish(tail_sum)
-    tail_low[...] = tail_sum[...].astype(BF16)
-    gather = Gather(place, tail_low, tail_o, gsend_sem, grecv_sem, gown_sem)
-    gather.start()
+    small.start()
+    small.run()
     reduce.finish(grad_o)
-    for away in range(1, line):
-        gather.column(away)
-        gather.square(away - 1)
-    gather.square(line - 1)
-    for away in range(line):
-        gather.corner(away)
-    for flip_x in range(2):
-        for flip_y in range(2):
-            for away in range(line):
-                for dist, level, test, way in place.levels():
-                    if dist == away:
-                        only(test, lambda: gather.partner(flip_x, flip_y, level))
-    gather.own.wait()
-    gather.wires.finish()
+    small.finish()
 
 
 def run_backward(
@@ -1448,10 +1434,7 @@
     shapes = (
         ((packs, length, width), F32),
         ((rows, width), F32),
-        ((ex, dp, few, width), BF16),
-    )
-    slabs = lambda r: tuple(
-        (dims + (r, width), BF16) for dims in ((4, line), (4, line), (line,), (2, line), (2, line))
+        ((ex // line, dp, line, few, width), BF16),
     )
     scratch = (
         ((width, 3 * width), BF16),
@@ -1467,21 +1450,22 @@
         ((packs * length, 3 * width), BF16),
         ((length, 3 * width), F32),
         ((16, width), F32),
-        ((ex, dp, few, width), BF16),
-        ((few, width), F32),
+        ((ex // line, dp, line, few, width), BF16),
         ((few, width), BF16),
         *([((line, rows, width), BF16)] * 5),
-        *slabs(few),
-    )
-    reduce_sems = [dma((20 * line,)), dma((4, line)), dma((line,)), dma((2, line)), dma((2, line)), dma((4, line))]
+        ((4, line, few, width), BF16),
+        ((4, line, few, width), BF16),
+        ((3, line, few, width), BF16),
+        ((line, few, width), BF16),
+    )
+    small_sems = [dma((n,)) for n in (4, 4, 3, 3, line, line, line, line, 3, 3, 4, 4)]
     return pl.pallas_call(
         functools.partial(backward_kernel, line),
         out_shape=tuple(jax.ShapeDtypeStruct(*s) for s in shapes),
         in_specs=[away] + [here] * 9 + [away] * 5,
         out_specs=(here, here, here),
         scratch_shapes=[pltpu.VMEM(*s) for s in scratch]
-        + [dma((5, packs)), dma((2, line))] + [dma((line,))] * 6 + reduce_sems
-        + [dma((24 * line,)), dma((ex, dp)), dma],
+        + [dma((5, packs)), dma((2, line))] + [dma((line,))] * 6 + small_sems,
         compiler_params=pltpu.CompilerParams(
             collective_id=slot, has_side_effects=True, vmem_limit_bytes=VMEM_BYTES
         ),
@@ -1603,6 +1587,7 @@
         inner_master[0], inner_first[0], inner_second[0],
         down_master[0], down_first[0], down_second[0],
     )
+    tail = tail.reshape(-1, lax.axis_size("dp"), *tail.shape[3:])
     new = run_update(tail, grad, weights)
     return (block_out, patch_grad, *new[:12], *(value[None] for value in new[12:]))
 
@@ -1615,7 +1600,7 @@
     experts = inner_master.shape[0] * lax.axis_size("expert")
     entries = inner_master.shape[1] * inner_master.shape[2] + down_master.shape[1] * down_master.shape[2]
     weight_bytes = 2 * experts * entries * lax.axis_size("dp")
-    square = lax.axis_size("dp") == 4 and inner_master.shape[0] == 1 and lax.axis_size("expert") == experts
+    square = lax.axis_size("dp") == 4 and lax.axis_size("expert") == 8 and inner_master.shape[0] == 1 and lax.axis_size("expert") == experts
     return (fast if square and weight_bytes <= GATHER_LIMIT else local)(*args)
 
 

time: 246 us -> 233 us (0.947)
  Pallas kernels: 231 us -> 218 us
    pallas_call x1, Pallas kernels: 133 us -> 123 us  [run_forward(): pl.pallas_call(functools.partial(forward_kernel, line, cap), out_shape=tu...]
    pallas_call x1, Pallas kernels: 86.9 us -> 83.9 us  [run_backward(): pl.pallas_call(functools.partial(backward_kernel, line), out_shape=tuple(...]
where the time goes in v1:
time: 233 us
  Pallas kernels  218 us (94%)
  local copies, waits for them, and re-layouts  11.4 us (5%)
  other arithmetic  2.56 us (1%)
    pallas_call x1, Pallas kernels, run_forward(): pl.pallas_call(functools.partial(forward_kernel, line, cap), out_shape=tu...  123 us
    pallas_call x1, Pallas kernels, run_backward(): pl.pallas_call(functools.partial(backward_kernel, line), out_shape=tuple(...  83.9 us
    unnamed x18, local copies, waits for them, and re-layouts  11.3 us
    pallas_call x1, Pallas kernels, run_update(): pl.pallas_call(update_kernel, out_shape=tuple((jax.ShapeDtypeStruct(w.sha...  11 us

profile of v1, /device:TPU:0, one launch (start us, length us, event | category | flops | bytes accessed | tf_op | source)
XLA Modules:
  0.0 232.9 jit_solution(7078166463711901096)
XLA Ops:
  0.7 0.0 copy-start.1
  0.7 0.0 copy-start.2
  0.7 1.1 convert.9
  1.8 0.1 reshape_squeeze.4
  1.9 0.0 copy-done.1
  2.0 0.8 pad_maximum_fusion.shard
  2.8 0.0 copy-done.2
  2.8 0.6 convert_bitcast_fusion.router_w
  3.4 123.3 %forward.1 = (bf16[8,4,576,384]{3,2,1,0:T(8,128)(2,1)}, bf16[3,4,576,384]{3,2,1,0:T(8,128)(2,1)}, bf16[3,512,1152]{2,1,0:T(8,128)(2,1)}, bf16[3,3,4,384,256]{4,3...) custom-call(bf16[576,384]{1,0:T(8,128)(2,1)} %pad_maximum_fusion.sha, ...), custom_call_target="tpu_custom_call" | custom-call | tf_op jit(solution)/shard_map/forward/pallas_call | solution.py:1228
  126.7 0.0 copy-start.3
  126.7 0.0 copy-start.4
  126.7 83.9 %backward.1 = (f32[3,512,384]{2,1,0:T(8,128)}, f32[576,384]{1,0:T(8,128)}, bf16[2,4,4,64,384]{4,3,2,1,0:T(8,128)(2,1)}) custom-call(bf16[3,4,576,384]{3,2,1,0:T(8,128)(2,1)} %get-tuple-element.51.kept, bf16[3,512,384]{2,1,0:T(8,128)(2,1)} %patches.3, bf16[3,512,384]{2,1,0:T(8,128)(2,1)} %upstream.3, s32[3,1,512]{2,1,0:T(1,128)} %items.3, f32[384,1152]{1,0:T(8,128)} %qkv_w.5, ...), custom_call_target="tpu_custom_call" | custom-call | tf_op jit(solution)/shard_map/backward/pallas_call | solution.py:1462
  210.6 0.8 copy.44.router_w
  211.4 0.0 copy-done.3
  211.4 0.8 copy.45.router_f
  212.2 0.8 copy.46.router_s
  213.0 11.0 %update.1 = (f32[384,1152]{1,0:T(8,128)}, f32[384,1152]{1,0:T(8,128)}, f32[384,1152]{1,0:T(8,128)}, f32[384,384]{1,0:T(8,128)}, f32[384,384]{1,0:T(8,128)}, /*in...) custom-call(bf16[8,4,64,384]{3,2,1,0:T(8,128)(2,1)} %bitcast.21, ...), custom_call_target="tpu_custom_call" | custom-call | tf_op jit(solution)/shard_map/update/pallas_call | solution.py:1536
  224.0 0.0 copy-start
  224.0 1.8 copy.47
  225.8 1.6 copy.48
  227.4 1.6 copy.49
  229.1 2.4 %copy.52 = bf16[3,512,384]{2,1,0:T(8,128)(2,1)} copy(bf16[3,512,384]{2,1,0:T(8,128)(2,1)} %get-tuple-element.120) | data formatting | bytes 2359296
  231.5 0.0 copy-done
  231.5 1.4 copy.53
  (3 shorter events, 0.1 us)
Async XLA Ops:
  0.7 1.3 copy-start.1
  0.7 2.1 copy-start.2
  126.7 84.7 %copy-start.3 = (f32[384,8]{0,1:T(8,128)S(1)}, f32[384,8]{0,1:T(8,128)}, u32[]{:S(2)}) copy-start(f32[384,8]{0,1:T(8,128)} %param.34) | copy-start | bytes 36868
  126.7 85.5 %copy-start.4 = (f32[384,8]{0,1:T(8,128)S(1)}, f32[384,8]{0,1:T(8,128)}, u32[]{:S(2)}) copy-start(f32[384,8]{0,1:T(8,128)} %param.35) | copy-start | bytes 36868
  224.0 7.4 %copy-start = (f32[3,512,384]{2,1,0:T(8,128)S(1)}, f32[3,512,384]{2,1,0:T(8,128)}, u32[]{:S(2)}) copy-start(f32[3,512,384]{2,1,0:T(8,128)} %get-tuple-element.121) | copy-start | bytes 7077892

commit v2 on v1

--- a/solution.py
+++ b/solution.py
@@ -667,8 +667,9 @@
 
 
 class Small:
-    def __init__(self, place, part, low, out, sums, core_in, square_in, line_in, sems):
-        self.place, self.part, self.low, self.out = place, part, low, out
+    def __init__(self, place, rows, part, low, out, sums, core_in, square_in, line_in, sems):
+        self.place, self.rows = place, rows
+        self.part, self.low, self.out = part, low, out
         self.sums, self.core_in, self.square_in, self.line_in = sums, core_in, square_in, line_in
         (
             self.core_send, self.core_sem, self.square_send, self.square_sem, self.line_send, self.line_sem,
@@ -688,50 +689,53 @@
     def core(self, group):
         y, d = self.lane(group, 1)
         return remote(
-            self.part.at[y, d], self.core_in.at[group], self.core_send.at[group], self.core_sem.at[group],
+            self.part.at[y, d, :, self.rows], self.core_in.at[group, :, self.rows], self.core_send.at[group], self.core_sem.at[group],
             self.place.device(0, 0, 1),
         )
 
     def over(self, group):
         return remote(
-            self.sums.at[group], self.square_in.at[group - 1], self.square_send.at[group - 1],
+            self.sums.at[group, :, self.rows], self.square_in.at[group - 1, :, self.rows], self.square_send.at[group - 1],
             self.square_sem.at[group - 1], self.to(group),
         )
 
     def along(self, z):
         return remote(
-            self.sums.at[OWN, z], self.line_in.at[self.place.z], self.line_send.at[z],
+            self.sums.at[OWN, z, self.rows], self.line_in.at[self.place.z, self.rows], self.line_send.at[z],
             self.line_sem.at[self.place.z], self.place.device(z=z),
         )
 
     def landed(self, z):
         return remote(
-            self.sums.at[OWN, z], self.line_in.at[z], self.line_send.at[z], self.line_sem.at[z],
+            self.sums.at[OWN, z, self.rows], self.line_in.at[z, self.rows], self.line_send.at[z], self.line_sem.at[z],
             self.place.device(z=z),
         )
 
     def up(self, z):
         y, d = self.lane(OWN)
         return remote(
-            self.low, self.out.at[y, d, self.place.z], self.up_send.at[z], self.up_sem.at[self.place.z],
+            self.low.at[self.rows], self.out.at[y, d, self.place.z, self.rows], self.up_send.at[z], self.up_sem.at[self.place.z],
             self.place.device(z=z),
         )
 
     def risen(self, z):
         y, d = self.lane(OWN)
-        return remote(self.low, self.out.at[y, d, z], self.up_send.at[z], self.up_sem.at[z], self.place.device(z=z))
+        return remote(
+            self.low.at[self.rows], self.out.at[y, d, z, self.rows], self.up_send.at[z], self.up_sem.at[z],
+            self.place.device(z=z),
+        )
 
     def back(self, group):
         y, d = self.lane(OWN)
         return remote(
-            self.out.at[y, d], self.out.at[y, d], self.back_send.at[group - 1], self.back_sem.at[group - 1],
+            self.out.at[y, d, :, self.rows], self.out.at[y, d, :, self.rows], self.back_send.at[group - 1], self.back_sem.at[group - 1],
             self.to(group),
         )
 
     def last(self, group):
         y, d = self.lane(group)
         return remote(
-            self.out.at[y, d], self.out.at[y, d], self.last_send.at[group], self.last_sem.at[group],
+            self.out.at[y, d, :, self.rows], self.out.at[y, d, :, self.rows], self.last_send.at[group], self.last_sem.at[group],
             self.place.device(0, 0, 1),
         )
 
@@ -742,42 +746,49 @@
         for group in (ACROSS, OVER_X, OVER_Y, OWN):
             self.core(group).start()
 
-    def run(self):
-        place = self.place
+    def stages(self):
+        place, rows = self.place, self.rows
         for group in (ACROSS, OVER_X, OVER_Y, OWN):
             self.core(group).wait_recv()
-            total = self.part[self.lane(group)].astype(F32) + self.core_in[group].astype(F32)
-            self.sums[group] = total.astype(BF16)
+            y, d = self.lane(group)
+            total = self.part[y, d, :, rows].astype(F32) + self.core_in[group, :, rows].astype(F32)
+            self.sums[group, :, rows] = total.astype(BF16)
             if group != OWN:
                 self.over(group).start()
-        total = self.sums[OWN].astype(F32)
+        yield
+        total = self.sums[OWN, :, rows].astype(F32)
         for group in (OVER_X, OVER_Y, ACROSS):
             self.over(group).wait_recv()
-            total = total + self.square_in[group - 1].astype(F32)
-        self.sums[OWN] = total.astype(BF16)
+            total = total + self.square_in[group - 1, :, rows].astype(F32)
+        self.sums[OWN, :, rows] = total.astype(BF16)
         for z in self.others():
             self.along(z).start()
-        total = self.sums[OWN, place.z].astype(F32)
+        yield
+        total = self.sums[OWN, place.z, rows].astype(F32)
         for z in self.others():
             self.landed(z).wait_recv()
-            total = total + self.line_in[z].astype(F32)
-        self.low[...] = total.astype(BF16)
+            total = total + self.line_in[z, rows].astype(F32)
+        self.low[rows] = total.astype(BF16)
         for z in self.others():
             self.up(z).start()
         y, d = self.lane(OWN)
-        self.out[y, d, place.z] = total.astype(BF16)
+        self.out[y, d, place.z, rows] = total.astype(BF16)
+        yield
         for z in self.others():
             self.risen(z).wait_recv()
         for group in (ACROSS, OVER_X, OVER_Y):
             self.back(group).start()
         self.last(OWN).start()
-
-    def finish(self):
+        yield
         for group in (OVER_X, OVER_Y, ACROSS):
             self.back(group).wait_recv()
             self.last(group).start()
+        yield
         for group in (OWN, OVER_X, OVER_Y, ACROSS):
             self.last(group).wait_recv()
+        yield
+
+    def finish(self):
         for group in (OWN, OVER_X, OVER_Y, ACROSS):
             self.core(group).wait_send()
             self.last(group).wait_send()
@@ -985,12 +996,12 @@
         for n in range(len(saves)):
             save(n, p).start()
         work.prepare(p, ids, router_w)
-        for k in range(1, line):
+        for k in range(1, line - 1):
 
             def relay(k=k):
                 gather.column(k)
-                if k != 2:
-                    gather.square(k // 2)
+                if k == 1:
+                    gather.square(0)
 
             pl.when(p == min(k - 1, packs - 1))(relay)
         return carry
@@ -1089,9 +1100,14 @@
         gather.corner(0)
         gather.corner(1)
 
+    def third():
+        gather.column(line - 1)
+        gather.square(1)
+
     events = (
-        (1, 0, lambda: gather.square(line - 2)),
-        (2, 0, last_square),
+        (0, 0, third),
+        (1, 1, lambda: gather.square(line - 2)),
+        (2, 1, last_square),
         (3, 0, two_corners),
         (3, 1, lambda: gather.corner(line - 2)),
         (3, packs - 1, lambda: gather.corner(line - 1)),
@@ -1363,7 +1379,14 @@
         place, kept, owns, sides, diag_in, side_in, line_in, own_sem,
         (diag_send, diag_sem, side_send, side_sem, line_send, line_sem),
     )
-    small = Small(place, tail, tail_low, tail_o, tsums, tcore_in, tsquare_in, tline_in, small_sems)
+    half = tail_low.shape[0] // 2
+    smalls = [
+        Small(
+            place, pl.ds(n * half, half), tail, tail_low, tail_o, tsums, tcore_in, tsquare_in, tline_in,
+            small_sems[12 * n : 12 * n + 12],
+        )
+        for n in range(2)
+    ]
     reduce.start()
     loads = ((mixed_i, mixed), (mid_i, mid), (nm_i, nm), (probs_i, probs), (att_i, att))
 
@@ -1415,10 +1438,15 @@
 
     lax.fori_loop(0, packs, pack, 0)
     work.tail(att, tail)
-    small.start()
-    small.run()
+    for small in smalls:
+        small.start()
+    chains = [small.stages() for small in smalls]
+    for stage in range(6):
+        for chain in chains:
+            next(chain)
     reduce.finish(grad_o)
-    small.finish()
+    for small in smalls:
+        small.finish()
 
 
 def run_backward(
@@ -1458,7 +1486,7 @@
         ((3, line, few, width), BF16),
         ((line, few, width), BF16),
     )
-    small_sems = [dma((n,)) for n in (4, 4, 3, 3, line, line, line, line, 3, 3, 4, 4)]
+    small_sems = [dma((n,)) for n in (4, 4, 3, 3, line, line, line, line, 3, 3, 4, 4) * 2]
     return pl.pallas_call(
         functools.partial(backward_kernel, line),
         out_shape=tuple(jax.ShapeDtypeStruct(*s) for s in shapes),
@@ -1483,7 +1511,7 @@
     step = pl.program_id(0)
     ex, dp, few, width = tail.shape
     rows = few - 16
-    experts = router_w.shape[1]
+    experts = router_w.shape[0]
     attn = tail[:, :, :rows, :].reshape(ex * dp * rows, width).astype(F32)
 
     def write(outs, values):
@@ -1498,7 +1526,7 @@
 
     def rest():
         small = tail[0, 0, rows:, :].astype(F32)
-        router_g = small.T[:, :experts]
+        router_g = small[:experts]
         gains_g = small[experts : experts + 2]
         write(
             (router_wo, router_fo, router_so),
@@ -1582,14 +1610,17 @@
     weights = (
         qkv_master, qkv_first, qkv_second,
         proj_master, proj_first, proj_second,
-        router_master, router_first, router_second,
+        router_master.T, router_first.T, router_second.T,
         gains_master, gains_first, gains_second,
         inner_master[0], inner_first[0], inner_second[0],
         down_master[0], down_first[0], down_second[0],
     )
     tail = tail.reshape(-1, lax.axis_size("dp"), *tail.shape[3:])
     new = run_update(tail, grad, weights)
-    return (block_out, patch_grad, *new[:12], *(value[None] for value in new[12:]))
+    return (
+        block_out, patch_grad, *new[:6], *(value.T for value in new[6:9]), *new[9:12],
+        *(value[None] for value in new[12:]),
+    )
 
 
 GATHER_LIMIT = 16 * 1024 * 1024

time: 233 us -> 225 us (0.966)
  local copies, waits for them, and re-layouts: 11.4 us -> 4.07 us
  Pallas kernels: 218 us -> 215 us
    unnamed x18 -> x4, local copies, waits for them, and re-layouts: 11.3 us -> 3.96 us
    pallas_call x1, Pallas kernels: 83.9 us -> 81.2 us  [run_backward(): pl.pallas_call(functools.partial(backward_kernel, line), out_shape=tuple(...]
where the time goes in v2:
time: 225 us; the launch traced here: 224 us
  Pallas kernels  215 us (96%)
  other arithmetic  4.19 us (2%)
  local copies, waits for them, and re-layouts  4.07 us (2%)
    pallas_call x1, Pallas kernels, run_forward(): pl.pallas_call(functools.partial(forward_kernel, line, cap), out_shape=tu...  123 us
    pallas_call x1, Pallas kernels, run_backward(): pl.pallas_call(functools.partial(backward_kernel, line), out_shape=tuple(...  81.2 us
    pallas_call x1, Pallas kernels, run_update(): pl.pallas_call(update_kernel, out_shape=tuple((jax.ShapeDtypeStruct(w.sha...  10.6 us

profile of v2, /device:TPU:0, one launch (start us, length us, event | category | flops | bytes accessed | tf_op | source)
XLA Modules:
  0.0 224.2 jit_solution(7712088349698660805)
XLA Ops:
  0.7 1.3 bitcast_convert_fusion.router_w
  2.0 1.0 bitcast_convert_fusion.1
  2.9 1.1 convert.9
  4.0 0.1 reshape_squeeze.4
  4.2 0.8 pad_maximum_fusion.shard
  5.0 123.4 %forward.1 = (bf16[8,4,576,384]{3,2,1,0:T(8,128)(2,1)}, bf16[3,4,576,384]{3,2,1,0:T(8,128)(2,1)}, bf16[3,512,1152]{2,1,0:T(8,128)(2,1)}, bf16[3,3,4,384,256]{4,3...) custom-call(bf16[576,384]{1,0:T(8,128)(2,1)} %pad_maximum_fusion.sha, ...), custom_call_target="tpu_custom_call" | custom-call | tf_op jit(solution)/shard_map/forward/pallas_call | solution.py:1244
  128.4 81.2 %backward.1 = (f32[3,512,384]{2,1,0:T(8,128)}, f32[576,384]{1,0:T(8,128)}, bf16[2,4,4,64,384]{4,3,2,1,0:T(8,128)(2,1)}) custom-call(bf16[3,4,576,384]{3,2,1,0:T(8,128)(2,1)} %get-tuple-element.51.kept, bf16[3,512,384]{2,1,0:T(8,128)(2,1)} %patches.3, bf16[3,512,384]{2,1,0:T(8,128)(2,1)} %upstream.3, s32[3,1,512]{2,1,0:T(1,128)} %items.3, f32[384,1152]{1,0:T(8,128)} %qkv_w.5, ...), custom_call_target="tpu_custom_call" | custom-call | tf_op jit(solution)/shard_map/backward/pallas_call | solution.py:1490
  209.6 10.6 %update.1 = (f32[384,1152]{1,0:T(8,128)}, f32[384,1152]{1,0:T(8,128)}, f32[384,1152]{1,0:T(8,128)}, f32[384,384]{1,0:T(8,128)}, f32[384,384]{1,0:T(8,128)}, /*in...) custom-call(bf16[8,4,64,384]{3,2,1,0:T(8,128)(2,1)} %bitcast.26, ...), custom_call_target="tpu_custom_call" | custom-call | tf_op jit(solution)/shard_map/update/pallas_call | solution.py:1564
  220.2 0.0 copy-start
  220.2 2.6 %copy.46 = bf16[3,512,384]{2,1,0:T(8,128)(2,1)} copy(bf16[3,512,384]{2,1,0:T(8,128)(2,1)} %get-tuple-element.100) | data formatting | bytes 2359296
  222.8 0.0 copy-done
  222.8 1.4 copy.47
  (1 shorter events, 0.0 us)
Async XLA Ops:
  220.2 2.6 %copy-start = (f32[3,512,384]{2,1,0:T(8,128)S(1)}, f32[3,512,384]{2,1,0:T(8,128)}, u32[]{:S(2)}) copy-start(f32[3,512,384]{2,1,0:T(8,128)} %get-tuple-element.101) | copy-start | bytes 7077892

commit v3 on v2

--- a/solution.py
+++ b/solution.py
@@ -962,7 +962,7 @@
     shard, patches, upstream, items, ids, qkv_w, proj_w, router_w, gains, table,
     full, kept_o, mixed_o, probs_o, att_o, mid_o, nm_o, block_o, gmid_o, glog_o,
     qkv_s, proj_s, mixed_s, probs_s, att_s, mid_s, nm_s, wbuf, pbuf,
-    rank_s, gate_s, gg_s, x_s, hid_s, go_s, gb_s, y_s, inner_s, down_s,
+    rank_s, gate_s, gg_s, x_s, hid_s, go_s, gb_s, y_s, inner_s, down_s, block_s, gmid_s,
     sums, core_in, diag_in, side_in,
     send_sem, recv_sem, own_sem, save_sem, fetch_sem, keep_sem,
     core_send, core_sem, diag_send, diag_sem, side_send, side_sem, credit_sem,
@@ -979,12 +979,16 @@
         (nm_s, upstream, rank_s, gate_s, gg_s, x_s, hid_s, go_s, gb_s, y_s, inner_s, down_s), cap
     )
     saves = ((mixed_s, mixed_o), (probs_s, probs_o), (att_s, att_o), (mid_s, mid_o), (nm_s, nm_o))
+    results = ((block_s, block_o), (gmid_s, gmid_o))
 
     def save(n, p):
         source, target = saves[n]
         return pltpu.make_async_copy(
             source.at[lax.rem(p, source.shape[0])], target.at[p], save_sem.at[n, p]
         )
+
+    def result(n, p):
+        return pltpu.make_async_copy(results[n][0].at[p], results[n][1].at[p], save_sem.at[len(saves) + n, p])
 
     def pack(p, carry):
         def reuse():
@@ -1153,7 +1157,9 @@
     lax.fori_loop(experts - 1, experts, last, 0)
 
     def finish(p, carry):
-        work.finish(p, router_w, mid_s, block_o, gmid_o, glog_o)
+        work.finish(p, router_w, mid_s, block_s, gmid_s, glog_o)
+        for n in range(len(results)):
+            result(n, p).start()
         return carry
 
     lax.fori_loop(0, packs, finish, 0)
@@ -1189,6 +1195,9 @@
     for n in range(len(saves)):
         for p in range(packs - 2 if n < 2 else 0, packs):
             save(n, p).wait()
+    for n in range(len(results)):
+        for p in range(packs):
+            result(n, p).wait()
     gather.wires.finish()
 
 
@@ -1236,6 +1245,8 @@
         ((packs, experts * cap, 2 * width), BF16),
         ((width, 2 * hidden), BF16),
         ((hidden, width), BF16),
+        ((packs, length, width), BF16),
+        ((packs, length, width), F32),
         ((4, line, rows, width), BF16),
         ((2, 2, rows, width), BF16),
         ((EARLY, rows, width), BF16),
@@ -1245,9 +1256,9 @@
         functools.partial(forward_kernel, line, cap),
         out_shape=tuple(jax.ShapeDtypeStruct(*s) for s in shapes),
         in_specs=[here] * 10,
-        out_specs=(away,) * 7 + (here,) * 3,
+        out_specs=(away,) * 9 + (here,),
         scratch_shapes=[pltpu.VMEM(*s) for s in scratch]
-        + [dma((24 * line,)), dma((ex, dp)), dma, dma((5, packs)), dma((2,)), dma((3, line))]
+        + [dma((24 * line,)), dma((ex, dp)), dma, dma((7, packs)), dma((2,)), dma((3, line))]
         + [dma((2, 2))] * 2 + [dma((EARLY,))] * 2 + [dma((line,))] * 2 + [pltpu.SemaphoreType.REGULAR],
         compiler_params=pltpu.CompilerParams(
             collective_id=slot, has_side_effects=True, vmem_limit_bytes=VMEM_BYTES
@@ -1265,7 +1276,7 @@
         ) = refs
 
     def pack(self, p, midway):
-        packs, length, width = self.patches.shape
+        packs, length, width = self.patch_o.shape
         pairs = width // 128
         experts = self.glog.shape[1]
         gains, mixed, dkv_s = self.gains, self.mixed, self.dkv_s
@@ -1275,17 +1286,17 @@
         mask_b = jnp.where(first_head, 0.0, 1.0).astype(BF16)
         top_rows = iota((128, 1), 0) < HEAD
         rows = pl.ds(pl.multiple_of(p * length, length), length)
-        source = self.patches[p].astype(F32)
+        slot = lax.rem(p, 2)
+        source = self.patches[slot].astype(F32)
         gain0, gain1 = gains[0:1, :], gains[1:2, :]
-        slot = lax.rem(p, 2)
         middle = self.mid[slot]
         inv = row_norm(middle)
         unit = middle * inv
-        grad_mid = self.gmid[p]
+        grad_mid = self.gmid[slot]
         self.small_g[experts + 1 : experts + 2, :] += jnp.sum(grad_mid * unit, axis=0, keepdims=True)
         self.small_g[0:experts, :] += dot_nn(self.glog[p], self.nm[slot])
         grad_unit = grad_mid * gain1
-        grad_middle = self.upstream[p].astype(F32) + inv * (
+        grad_middle = self.upstream[slot].astype(F32) + inv * (
             grad_unit - unit * jnp.mean(grad_unit * unit, axis=1, keepdims=True)
         )
         self.patch_o[p] = grad_middle
@@ -1335,7 +1346,7 @@
         )
 
     def tail(self, att, tail):
-        packs, length, width = self.patches.shape
+        packs, length, width = self.patch_o.shape
         tail[...] = jnp.zeros(tail.shape, BF16)
         for block in range(4):
             if block < 3:
@@ -1363,16 +1374,16 @@
 
 def backward_kernel(
     line,
-    kept, patches, upstream, items, qkv_w, proj_w, gains, table, gmid, glog, mixed_i, probs_i, att_i, mid_i, nm_i,
+    kept, patches_i, upstream_i, items, qkv_w, proj_w, gains, table, gmid_i, glog, mixed_i, probs_i, att_i, mid_i, nm_i,
     patch_o, grad_o, tail_o,
-    qkv_s, proj_s, mixed, probs, att, mid, nm,
+    qkv_s, proj_s, mixed, probs, att, mid, nm, patches, upstream, gmid,
     normed_s, branch_s, datt_s, dmix_s, dkv_s, small_g, tail, tail_low,
     owns, sides, diag_in, side_in, line_in,
     tsums, tcore_in, tsquare_in, tline_in,
     load_sem, own_sem, diag_send, diag_sem, side_send, side_sem, line_send, line_sem,
     *small_sems,
 ):
-    packs = patches.shape[0]
+    packs = patch_o.shape[0]
     place = Place(line)
     place.greet()
     reduce = Close(
@@ -1388,7 +1399,10 @@
         for n in range(2)
     ]
     reduce.start()
-    loads = ((mixed_i, mixed), (mid_i, mid), (nm_i, nm), (probs_i, probs), (att_i, att))
+    loads = (
+        (gmid_i, gmid), (mid_i, mid), (nm_i, nm), (upstream_i, upstream), (patches_i, patches),
+        (mixed_i, mixed), (probs_i, probs), (att_i, att),
+    )
 
     def load(n, p):
         source, target = loads[n]
@@ -1472,6 +1486,9 @@
         (att.shape, BF16),
         ((2,) + mid.shape[1:], F32),
         ((2,) + nm.shape[1:], BF16),
+        ((2, length, width), BF16),
+        ((2, length, width), BF16),
+        ((2, length, width), F32),
         ((packs * length, width), BF16),
         ((packs * length, width), BF16),
         ((length, width), BF16),
@@ -1490,10 +1507,10 @@
     return pl.pallas_call(
         functools.partial(backward_kernel, line),
         out_shape=tuple(jax.ShapeDtypeStruct(*s) for s in shapes),
-        in_specs=[away] + [here] * 9 + [away] * 5,
+        in_specs=[away] * 3 + [here] * 5 + [away, here] + [away] * 5,
         out_specs=(here, here, here),
         scratch_shapes=[pltpu.VMEM(*s) for s in scratch]
-        + [dma((5, packs)), dma((2, line))] + [dma((line,))] * 6 + small_sems,
+        + [dma((8, packs)), dma((2, line))] + [dma((line,))] * 6 + small_sems,
         compiler_params=pltpu.CompilerParams(
             collective_id=slot, has_side_effects=True, vmem_limit_bytes=VMEM_BYTES
         ),

time: 225 us -> 223 us (level)
  no operation moved by 1% of the time
where the time goes in v3:
time: 223 us; the launch traced here: 222 us
  Pallas kernels  213 us (96%)
  other arithmetic  4.19 us (2%)
  local copies, waits for them, and re-layouts  4.07 us (2%)
    pallas_call x1, Pallas kernels, run_forward(): pl.pallas_call(functools.partial(forward_kernel, line, cap), out_shape=tu...  122 us
    pallas_call x1, Pallas kernels, run_backward(): pl.pallas_call(functools.partial(backward_kernel, line), out_shape=tuple(...  79.9 us
    pallas_call x1, Pallas kernels, run_update(): pl.pallas_call(update_kernel, out_shape=tuple((jax.ShapeDtypeStruct(w.sha...  10.6 us

profile of v3, /device:TPU:0, one launch (start us, length us, event | category | flops | bytes accessed | tf_op | source)
XLA Modules:
  0.0 221.9 jit_solution(3017225084929186382)
XLA Ops:
  0.7 1.3 bitcast_convert_fusion.router_w
  2.0 1.0 bitcast_convert_fusion.1
  2.9 1.1 convert.9
  4.0 0.1 reshape_squeeze.4
  4.2 0.8 pad_maximum_fusion.shard
  5.0 122.5 %forward.1 = (bf16[8,4,576,384]{3,2,1,0:T(8,128)(2,1)}, bf16[3,4,576,384]{3,2,1,0:T(8,128)(2,1)}, bf16[3,512,1152]{2,1,0:T(8,128)(2,1)}, bf16[3,3,4,384,256]{4,3...) custom-call(bf16[576,384]{1,0:T(8,128)(2,1)} %pad_maximum_fusion.sha, ...), custom_call_target="tpu_custom_call" | custom-call | tf_op jit(solution)/shard_map/forward/pallas_call | solution.py:1255
  127.4 79.9 %backward.1 = (f32[3,512,384]{2,1,0:T(8,128)}, f32[576,384]{1,0:T(8,128)}, bf16[2,4,4,64,384]{4,3,2,1,0:T(8,128)(2,1)}) custom-call(bf16[3,4,576,384]{3,2,1,0:T(8,128)(2,1)} %get-tuple-element.51.kept, bf16[3,512,384]{2,1,0:T(8,128)(2,1)} %patches_i.1, bf16[3,512,384]{2,1,0:T(8,128)(2,1)} %upstream_i.1, s32[3,1,512]{2,1,0:T(1,128)} %items.3, ...), custom_call_target="tpu_custom_call" | custom-call | tf_op jit(solution)/shard_map/backward/pallas_call | solution.py:1507
  207.4 10.6 %update.1 = (f32[384,1152]{1,0:T(8,128)}, f32[384,1152]{1,0:T(8,128)}, f32[384,1152]{1,0:T(8,128)}, f32[384,384]{1,0:T(8,128)}, f32[384,384]{1,0:T(8,128)}, /*in...) custom-call(bf16[8,4,64,384]{3,2,1,0:T(8,128)(2,1)} %bitcast.26, ...), custom_call_target="tpu_custom_call" | custom-call | tf_op jit(solution)/shard_map/update/pallas_call | solution.py:1581
  218.0 0.0 copy-start
  218.0 2.6 %copy.46 = bf16[3,512,384]{2,1,0:T(8,128)(2,1)} copy(bf16[3,512,384]{2,1,0:T(8,128)(2,1)} %get-tuple-element.100) | data formatting | bytes 2359296
  220.5 0.0 copy-done
  220.5 1.4 copy.47
  (1 shorter events, 0.0 us)
Async XLA Ops:
  218.0 2.6 %copy-start = (f32[3,512,384]{2,1,0:T(8,128)S(1)}, f32[3,512,384]{2,1,0:T(8,128)}, u32[]{:S(2)}) copy-start(f32[3,512,384]{2,1,0:T(8,128)} %get-tuple-element.101) | copy-start | bytes 7077892
